TPU v7x, 256 devices: a whole 4x4x8 slice. The times are simulated.
256 devices in a mesh: seq: 128 (over z, y_hi, x, core), head: 2 (over y_lo).
Axes of the slice: x: 4, y: 4 (y_hi: 2, y_lo: 2; y = y_hi * 2 + y_lo), z: 8, core: 2. Of those that a mesh axis runs over, the one named last changes fastest.
Arguments:
- queries: bfloat16 [16384, 2048], P(('seq', 'head')), may hold values from -8 to 8
- key_rows: bfloat16 [16384, 2048], P(('seq', 'head')), may hold values from -8 to 8
- values: bfloat16 [16384, 2048], P(('seq', 'head')), may hold values from -6 to 6
- out_grad: bfloat16 [16384, 2048], P(('seq', 'head')), may hold values from -6 to 6
Outputs:
- attended: bfloat16 [16384, 2048], P(('seq', 'head'))
- query_grad: bfloat16 [16384, 2048], P(('seq', 'head'))
- key_grad: bfloat16 [16384, 2048], P(('seq', 'head'))
- value_grad: bfloat16 [16384, 2048], P(('seq', 'head'))
All inputs are finite; a program needn't handle non-finite values.
Results may differ from a plain program's by a relative error of at most 0.028.
Values may be sent and summed in bfloat16 or wider, within the bound.
A program may use at most 64 MiB of HBM per device.

v0:
```python
import math

import jax
import jax.numpy as jnp
from jax import lax
from jax.sharding import PartitionSpec as P

HEAD_DIM = 128


ROOT_HALF = 0.7071067811865476


def swapped(block, axis, distance):
    count = lax.axis_size(axis)
    route = []
    for low in range(count):
        high = low | 1 << distance
        if high != low and high < count:
            route += [(low, high), (high, low)]
    return lax.ppermute(block, axis, route)


def pool_rows(blocks):
    widened = blocks.astype(jnp.float32)
    paired = widened.reshape((widened.shape[0] // 2, 2) + widened.shape[1:])
    return ((paired[:, 0] + paired[:, 1]) * ROOT_HALF).astype(jnp.bfloat16)


def unpool_rows(blocks):
    return jnp.repeat(blocks, 2, axis=0) * ROOT_HALF


def local(queries, key_rows, values, out_grad):
    query_in, key_in, value_in, grad_in = (
        lax.all_to_all(queries, "head", split_axis=1, concat_axis=0, tiled=True),
        lax.all_to_all(key_rows, "head", split_axis=1, concat_axis=0, tiled=True),
        lax.all_to_all(values, "head", split_axis=1, concat_axis=0, tiled=True),
        lax.all_to_all(out_grad, "head", split_axis=1, concat_axis=0, tiled=True),
    )
    token_rows = query_in.shape[0]
    head_count = query_in.shape[1] // HEAD_DIM
    local_shape = (token_rows, head_count, HEAD_DIM)
    query_loc = query_in.reshape(local_shape)
    key_loc = key_in.reshape(local_shape)
    value_loc = value_in.reshape(local_shape)
    grad_loc = grad_in.reshape(local_shape)
    level_count = lax.axis_size("seq").bit_length() - 1
    seq_index = lax.axis_index("seq")
    half_rows = token_rows // 2
    scale_factor = 1.0 / math.sqrt(HEAD_DIM)
    top_bit = seq_index >> level_count - 1 & 1
    sibling_start = (1 - top_bit) * half_rows
    query_pool = [query_loc]
    key_pool = [key_loc]
    value_pool = [value_loc]
    for level_no in range(1, level_count + 1):
        query_pool.append(pool_rows(query_pool[-1]))
        key_pool.append(pool_rows(key_pool[-1]))
        value_pool.append(pool_rows(value_pool[-1]))
    own_keys = key_pool[1]
    own_values = value_pool[1]
    records = []
    for level_no in range(1, level_count + 1):
        if level_no < level_count:
            sib_keys, sib_values = swapped((own_keys, own_values), "seq", level_no - 1)
        else:
            whole_keys, whole_values = (
                lax.all_gather(key_pool[level_count], "seq", axis=0, tiled=True),
                lax.all_gather(value_pool[level_count], "seq", axis=0, tiled=True),
            )
            sib_keys = lax.dynamic_slice_in_dim(whole_keys, sibling_start, half_rows, 0)
            sib_values = lax.dynamic_slice_in_dim(whole_values, sibling_start, half_rows, 0)
        coarse_scores = (
            jnp.einsum(
                "ghd,chd->ghc", query_pool[level_no], sib_keys, preferred_element_type=jnp.float32
            )
            * scale_factor
        )
        coarse_top = jnp.max(coarse_scores, axis=-1)
        coarse_expo = jnp.exp(coarse_scores - coarse_top[..., None])
        coarse_total = jnp.sum(coarse_expo, axis=-1)
        expo_half = coarse_expo.astype(jnp.bfloat16)
        coarse_numer = jnp.einsum(
            "ghc,chd->ghd", expo_half, sib_values, preferred_element_type=jnp.float32
        )
        records.append(
            (sib_keys, sib_values, coarse_expo, expo_half, coarse_top, coarse_total, coarse_numer)
        )
        if level_no < level_count - 1:
            own_bit = seq_index >> level_no - 1 & 1
            lower_keys = jnp.where(own_bit == 0, own_keys, sib_keys)
            upper_keys = jnp.where(own_bit == 0, sib_keys, own_keys)
            lower_values = jnp.where(own_bit == 0, own_values, sib_values)
            upper_values = jnp.where(own_bit == 0, sib_values, own_values)
            own_keys = pool_rows(jnp.concatenate([lower_keys, upper_keys], axis=0))
            own_values = pool_rows(jnp.concatenate([lower_values, upper_values], axis=0))
    local_scores = (
        jnp.einsum("thd,uhd->thu", query_loc, key_loc, preferred_element_type=jnp.float32)
        * scale_factor
    )
    row_top = jnp.max(local_scores, axis=-1)
    for level_no in range(1, level_count + 1):
        row_top = jnp.maximum(row_top, jnp.repeat(records[level_no - 1][4], 2**level_no, axis=0))
    local_expo = jnp.exp(local_scores - row_top[..., None])
    row_total = jnp.sum(local_expo, axis=-1)
    numer_all = jnp.einsum(
        "thu,uhd->thd",
        local_expo.astype(jnp.bfloat16),
        value_loc,
        preferred_element_type=jnp.float32,
    )
    factors = []
    for level_no in range(1, level_count + 1):
        group_rows = 2**level_no
        record = records[level_no - 1]
        factor = jnp.exp(jnp.repeat(record[4], group_rows, axis=0) - row_top)
        row_total = row_total + factor * jnp.repeat(record[5], group_rows, axis=0)
        numer_all = numer_all + factor[..., None] * jnp.repeat(record[6], group_rows, axis=0)
        factors.append(factor)
    outcome = numer_all / row_total[..., None]
    attended = outcome.astype(jnp.bfloat16).reshape(token_rows, -1)
    grad_wide = grad_loc.astype(jnp.float32)
    row_dots = jnp.sum(grad_wide * outcome, axis=-1)
    local_probs = local_expo / row_total[..., None]
    local_dprob = jnp.einsum(
        "thd,uhd->thu", grad_loc, value_loc, preferred_element_type=jnp.float32
    )
    dlocal = (local_probs * (local_dprob - row_dots[..., None])).astype(jnp.bfloat16)
    query_acc = (
        jnp.einsum("thu,uhd->thd", dlocal, key_loc, preferred_element_type=jnp.float32)
        * scale_factor
    )
    key_acc = (
        jnp.einsum("thu,thd->uhd", dlocal, query_loc, preferred_element_type=jnp.float32)
        * scale_factor
    )
    value_acc = jnp.einsum(
        "thu,thd->uhd",
        local_probs.astype(jnp.bfloat16),
        grad_loc,
        preferred_element_type=jnp.float32,
    )
    level_grads = []
    for level_no in range(1, level_count + 1):
        sib_keys, sib_values, coarse_expo, expo_half = records[level_no - 1][:4]
        group_rows = 2**level_no
        coarse_rows = token_rows // group_rows
        weight = factors[level_no - 1] / row_total
        adjoint = (
            (weight[..., None] * grad_wide)
            .reshape(coarse_rows, group_rows, head_count, HEAD_DIM)
            .sum(axis=1)
            .astype(jnp.bfloat16)
        )
        offset = (weight * row_dots).reshape(coarse_rows, group_rows, head_count).sum(axis=1)
        inner_dot = (
            jnp.einsum("ghd,chd->ghc", adjoint, sib_values, preferred_element_type=jnp.float32)
            - offset[..., None]
        )
        dcoarse = (coarse_expo * inner_dot).astype(jnp.bfloat16)
        dquery_level = (
            jnp.einsum("ghc,chd->ghd", dcoarse, sib_keys, preferred_element_type=jnp.float32)
            * scale_factor
        )
        dkey_sib = (
            jnp.einsum(
                "ghc,ghd->chd", dcoarse, query_pool[level_no], preferred_element_type=jnp.float32
            )
            * scale_factor
        )
        dvalue_sib = jnp.einsum(
            "ghc,ghd->chd", expo_half, adjoint, preferred_element_type=jnp.float32
        )
        level_grads.append((dquery_level, dkey_sib, dvalue_sib))
    query_carry = jnp.zeros((token_rows >> level_count, head_count, HEAD_DIM), jnp.float32)
    for level_no in range(level_count, 0, -1):
        query_carry = unpool_rows(query_carry + level_grads[level_no - 1][0])
    query_total = query_acc + query_carry
    tail_keys = None
    tail_values = None
    own_grad_keys = None
    own_grad_values = None
    spread_keys = jnp.zeros(local_shape, jnp.float32)
    spread_values = jnp.zeros(local_shape, jnp.float32)
    spread_keys = lax.dynamic_update_slice_in_dim(spread_keys, level_grads[-1][1], sibling_start, 0)
    spread_values = lax.dynamic_update_slice_in_dim(
        spread_values, level_grads[-1][2], sibling_start, 0
    )
    tail_keys, tail_values = (
        lax.psum_scatter(spread_keys, "seq", scatter_dimension=0, tiled=True),
        lax.psum_scatter(spread_values, "seq", scatter_dimension=0, tiled=True),
    )
    for level_no in range(level_count - 1, 0, -1):
        send_keys = level_grads[level_no - 1][1]
        send_values = level_grads[level_no - 1][2]
        keep_keys = None
        keep_values = None
        if own_grad_keys is not None:
            own_bit = seq_index >> level_no - 1 & 1
            wide_keys = unpool_rows(own_grad_keys)
            wide_values = unpool_rows(own_grad_values)
            keep_keys = jnp.where(own_bit == 0, wide_keys[:half_rows], wide_keys[half_rows:])
            keep_values = jnp.where(own_bit == 0, wide_values[:half_rows], wide_values[half_rows:])
            send_keys = send_keys + jnp.where(
                own_bit == 0, wide_keys[half_rows:], wide_keys[:half_rows]
            )
            send_values = send_values + jnp.where(
                own_bit == 0, wide_values[half_rows:], wide_values[:half_rows]
            )
        recv_keys, recv_values = (
            swapped(send_keys.astype(jnp.bfloat16), "seq", level_no - 1).astype(send_keys.dtype),
            swapped(send_values.astype(jnp.bfloat16), "seq", level_no - 1).astype(
                send_values.dtype
            ),
        )
        if keep_keys is None:
            own_grad_keys = recv_keys
            own_grad_values = recv_values
        else:
            own_grad_keys = keep_keys + recv_keys
            own_grad_values = keep_values + recv_values
    for level_no in range(level_count, 1, -1):
        tail_keys = unpool_rows(tail_keys)
        tail_values = unpool_rows(tail_values)
    base_keys = tail_keys
    base_values = tail_values
    base_keys = base_keys + own_grad_keys
    base_values = base_values + own_grad_values
    key_total = key_acc + unpool_rows(base_keys)
    value_total = value_acc + unpool_rows(base_values)
    query_out = query_total.astype(jnp.bfloat16).reshape(token_rows, -1)
    key_out = key_total.astype(jnp.bfloat16).reshape(token_rows, -1)
    value_out = value_total.astype(jnp.bfloat16).reshape(token_rows, -1)
    return (
        lax.all_to_all(attended, "head", split_axis=0, concat_axis=1, tiled=True),
        lax.all_to_all(query_out, "head", split_axis=0, concat_axis=1, tiled=True),
        lax.all_to_all(key_out, "head", split_axis=0, concat_axis=1, tiled=True),
        lax.all_to_all(value_out, "head", split_axis=0, concat_axis=1, tiled=True),
    )


def solution(mesh):
    in_specs = (
        P(("seq", "head"), None),
        P(("seq", "head"), None),
        P(("seq", "head"), None),
        P(("seq", "head"), None),
    )
    out_specs = (
        P(("seq", "head"), None),
        P(("seq", "head"), None),
        P(("seq", "head"), None),
        P(("seq", "head"), None),
    )
    return jax.shard_map(local, mesh=mesh, in_specs=in_specs, out_specs=out_specs, check_vma=False)
```

profile of v0, /device:TPU:1, one launch (start us, length us, event | category | flops | bytes accessed | tf_op | source)
XLA Modules:
  0.0 1851.0 jit_solution(11937206118050483747)
XLA Ops:
  8.8 3.6 all-to-all-start.1
  17.1 3.4 all-to-all-start
  21.9 2.8 all-to-all-done
  24.7 3.4 all-to-all-start.2
  31.1 4.8 collective-permute-start
  36.6 3.5 all-to-all-start.4
  43.1 184.6 %all-gather = bf16[128,1,8,128]{3,2,1,0:T(8,128)(2,1)S(1)} all-gather(bf16[1,1,8,128]{3,2,1,0:T(8,128)(2,1)S(1)} %fusion.264), channel_id=2, replica_groups=mesh['seq'=128,'head'=2] {'seq'}, dimensions={0}, use_global_device_ids=true | all-gather | bytes 264192 | tf_op jit(solution)/shard_map/all_gather | solution.py:69
  228.2 175.9 %all-gather.1 = bf16[128,1,8,128]{3,2,1,0:T(8,128)(2,1)S(1)} all-gather(bf16[1,1,8,128]{3,2,1,0:T(8,128)(2,1)S(1)} %fusion.260), channel_id=3, replica_groups=mesh['seq'=128,'head'=2] {'seq'}, dimensions={0}, use_global_device_ids=true | all-gather | bytes 264192 | tf_op jit(solution)/shard_map/all_gather | solution.py:70
  431.3 2.9 collective-permute-start.8
  452.6 3.1 collective-permute-start.9
  481.9 2.6 collective-permute-start.11
  499.3 3.7 multiply_reduce_fusion.4
  547.4 4.2 all-to-all-start.5
  564.5 1.8 collective-permute-start.14
  571.1 1.9 collective-permute-start.15
  578.5 2.0 collective-permute-done.22
  581.0 7.6 collective-permute-start.23
  589.1 2.2 collective-permute-start.17
  591.3 1222.3 %all-reduce.5.cloned.1.call-done = (f32[128,8,128]{2,1,0:T(8,128)}, f32[128,8,128]{2,1,0:T(8,128)}) async-done(((f32[128,8,128]{2,1,0:T(8,128)}, f32[128,8,128]{2,1,0:T(8,128)}), (f32[128,8,128]{2,1,0:T(8,128)}, f32[128,8,128]{2,1,0:T(8,128)})) %all-reduce.5.cloned.1.call-update) | async-done | bytes 1048592
  1818.5 3.4 all-to-all-start.3
  1822.1 3.9 all-to-all-done.3
  1826.0 3.4 all-to-all-start.7
  1830.8 4.1 all-to-all-done.7
  1834.9 3.4 all-to-all-start.6
  (896 shorter events, 179.3 us)
Async XLA Ops:
  8.8 8.3 all-to-all-start.1
  24.7 11.9 all-to-all-start.2
  31.1 379.8 %collective-permute-start = (bf16[64,8,128]{2,0,1:T(8,128)(2,1)S(1)}, bf16[64,8,128]{2,0,1:T(8,128)(2,1)S(1)}, u32[]{:S(2)}, u32[]{:S(2)}) collective-permute-start(bf16[64,8,128]{2,0,1:T(8,128)(2,1)S(1)} %bitcast.781), channel_id=1, source_target_pairs={{0,2},{2,0},{4,6},{6,4},{8,10},{10,8},{12,14},{14,12},{16,18},{18,... | collective-permute-start | bytes 393224 | tf_op jit(solution)/shard_map/ppermute | solution.py:21
  36.6 369.2 %all-to-all-start.4 = ((bf16[64,2,1024]{2,0,1:T(8,128)(2,1)}), bf16[64,2,1024]{2,0,1:T(8,128)(2,1)S(1)}, u32[]{:S(2)}, u32[]{:S(2)}) async-start(bf16[64,2,1024]{2,0,1:T(8,128)(2,1)} %bitcast.706), calls=%async_computation.4 | async-start | bytes 524288 | tf_op jit(solution)/shard_map/all_to_all | solution.py:39
  40.3 370.6 %collective-permute-start.6 = (bf16[64,8,128]{2,0,1:T(8,128)(2,1)S(1)}, bf16[64,8,128]{2,0,1:T(8,128)(2,1)S(1)}, u32[]{:S(2)}, u32[]{:S(2)}) collective-permute-start(bf16[64,8,128]{2,0,1:T(8,128)(2,1)S(1)} %bitcast.783), channel_id=1, source_target_pairs={{0,2},{2,0},{4,6},{6,4},{8,10},{10,8},{12,14},{14,12},{16,18},{18,... | collective-permute-start | bytes 393224 | tf_op jit(solution)/shard_map/ppermute | solution.py:21
  411.5 13.3 collective-permute-start.1
  417.2 12.0 collective-permute-start.7
  425.4 16.3 collective-permute-start.2
  431.3 18.5 collective-permute-start.8
  449.8 8.6 collective-permute-start.3
  452.6 12.7 collective-permute-start.9
  465.2 7.7 collective-permute-start.4
  467.2 11.5 collective-permute-start.10
  478.7 10.2 collective-permute-start.5
  481.9 11.3 collective-permute-start.11
  518.4 36.4 %collective-permute-start.18 = (bf16[64,8,128]{2,0,1:T(8,128)(2,1)}, bf16[64,8,128]{2,0,1:T(8,128)(2,1)}, u32[]{:S(2)}, u32[]{:S(2)}) collective-permute-start(bf16[64,8,128]{2,0,1:T(8,128)(2,1)} %fusion.60), channel_id=1, source_target_pairs={{0,64},{64,0},{2,66},{66,2},{4,68},{68,4},{6,70},{70,6},{8,72},{72... | collective-permute-start | bytes 393224 | tf_op jit(solution)/shard_map/ppermute | solution.py:21
  532.6 24.3 %collective-permute-start.12 = (bf16[64,8,128]{2,0,1:T(8,128)(2,1)}, bf16[64,8,128]{2,0,1:T(8,128)(2,1)}, u32[]{:S(2)}, u32[]{:S(2)}) collective-permute-start(bf16[64,8,128]{2,0,1:T(8,128)(2,1)} %fusion.53), channel_id=1, source_target_pairs={{0,64},{64,0},{2,66},{66,2},{4,68},{68,4},{6,70},{70,6},{8,72},{72... | collective-permute-start | bytes 393224 | tf_op jit(solution)/shard_map/ppermute | solution.py:21
  547.4 1271.2 %all-to-all-start.5 = ((bf16[2,64,1024]{2,1,0:T(8,128)(2,1)}), bf16[2,64,1024]{2,1,0:T(8,128)(2,1)}, u32[]{:S(2)}, u32[]{:S(2)}) async-start(bf16[2,64,1024]{2,1,0:T(8,128)(2,1)} %all_to_all.120), calls=%async_computation.5 | async-start | bytes 524288 | tf_op jit(solution)/shard_map/all_to_all | solution.py:237
  551.6 1261.9 %all-reduce.5.cloned.1.call-start = ((), (), s32[]{:S(2)}) async-start(), calls=%async_computation.8 | async-start | bytes 2097152
  577.0 11.6 collective-permute-start.16
  581.0 1233.8 %collective-permute-start.23 = (bf16[64,8,128]{2,0,1:T(8,128)(2,1)S(1)}, bf16[64,8,128]{2,0,1:T(8,128)(2,1)S(1)}, u32[]{:S(2)}, u32[]{:S(2)}) collective-permute-start(bf16[64,8,128]{2,0,1:T(8,128)(2,1)S(1)} %fusion.46), channel_id=1, source_target_pairs={{0,2},{2,0},{4,6},{6,4},{8,10},{10,8},{12,14},{14,12},{16,18},{18,... | collective-permute-start | bytes 393224 | tf_op jit(solution)/shard_map/ppermute | solution.py:21
  589.1 1232.9 %collective-permute-start.17 = (bf16[64,8,128]{2,0,1:T(8,128)(2,1)S(1)}, bf16[64,8,128]{2,0,1:T(8,128)(2,1)S(1)}, u32[]{:S(2)}, u32[]{:S(2)}) collective-permute-start(bf16[64,8,128]{2,0,1:T(8,128)(2,1)S(1)} %fusion.48), channel_id=1, source_target_pairs={{0,2},{2,0},{4,6},{6,4},{8,10},{10,8},{12,14},{14,12},{16,18},{18,... | collective-permute-start | bytes 393224 | tf_op jit(solution)/shard_map/ppermute | solution.py:21
  1826.0 9.0 all-to-all-start.7
  1834.9 8.3 all-to-all-start.6
  (221 other events, 384.5 us)
Sparse Core Ops, SparseCore 0:
  555.1 1258.4 all-reduce.4
where the time goes:
time: 1870 us; the launch traced here: 1850 us
  waiting for transfers between devices  1240 us (66%)
  blocking collectives  360 us (19%)
  local copies, waits for them, and re-layouts  122 us (7%)
  starting transfers between devices  69.5 us (4%)
  other arithmetic  24.6 us (1%)
    unnamed x2, waiting for transfers between devices  1220 us
    all_gather x1, blocking collectives, local(): lax.all_gather(key_pool[level_count], 'seq', axis=0, tiled=True)  185 us
    all_gather x1, blocking collectives, local(): lax.all_gather(value_pool[level_count], 'seq', axis=0, tiled=True)  176 us
    ppermute x24, starting transfers between devices, swapped(): return lax.ppermute(block, axis, route)  41 us
  transfers between devices with their start and end apart: 33, of which 13 were waited for; matrix products, arithmetic and copies ran while one was open for 6% of the time, Pallas kernels for 0%

commit v1 on v0

v1 whole, which is shorter than its diff:
```python
import functools
import math

import jax
import jax.numpy as jnp
import numpy as np
from jax import lax
from jax.experimental import pallas as pl
from jax.experimental.pallas import tpu as pltpu
from jax.sharding import PartitionSpec as P

MESH = pl.DeviceIdType.MESH
BF16 = jnp.bfloat16
F32 = jnp.float32
DH = 128
SCALE = 1.0 / math.sqrt(DH)
ROOT_HALF = 0.7071067811865476
LOW = -1e30
FLOOR = -1e29

PARTNERS = [(1, 0, 0, 64)]
PARTNERS += [(n, 64, 64 + 32 * (n - 2), 32) for n in (2, 3)]
PARTNERS += [(n, 96, 128 + 16 * (n - 4), 16) for n in (4, 5, 6, 7)]


def tables():
    level_of = np.zeros(128, np.int64)
    pool = np.zeros((128, 128), np.float32)
    row = 0
    for level in range(1, 8):
        for i in range(128 >> level):
            pool[row, i << level : (i + 1) << level] = 1.0
            level_of[row] = level
            row += 1
    level_of[127] = 99
    stage = np.zeros((128, 256), np.float32)
    stage_scale = np.ones(128, np.float32)
    for level, start, count in ((5, 0, 64), (6, 64, 32), (7, 96, 16)):
        per_chip = count // 8
        for r in range(count):
            chip, i = r // per_chip, r % per_chip
            if chip == 0:
                base, have = 192, 4
            elif chip == 1:
                base, have = 0, 2
            elif chip < 4:
                base, have = 64 + 32 * (chip - 2), 3
            else:
                base, have = 128 + 16 * (chip - 4), 4
            span = 1 << (level - have)
            stage[start + r, base + i * span : base + (i + 1) * span] = 1.0
            stage_scale[start + r] = 2.0 ** (-(level - have) / 2)
    fold = np.zeros((64, 256), np.float32)
    for r in range(64):
        fold[r, r] = 1.0
        for j in range(2):
            fold[r, 64 + 32 * j + r // 2] = 2.0**-0.5
        for j in range(4):
            fold[r, 128 + 16 * j + r // 4] = 0.5
    spread = np.zeros((192, 256), np.float32)
    for r in range(64):
        spread[r, 8 + r // 8] = 2.0**-1.5
    for r in range(64):
        spread[64 + r, 16 + r // 4] = 0.5
        spread[128 + r, 32 + r // 2] = 2.0**-0.5
    unfold = np.zeros((128, 256), np.float32)
    for r in range(128):
        unfold[r, r // 2] = 2.0**-0.5
        for j in range(2):
            unfold[r, 64 + 32 * j + r // 4] = 0.5
        for j in range(4):
            unfold[r, 128 + 16 * j + r // 8] = 2.0**-1.5
        unfold[r, 192 + r // 16] = 0.25
    last = np.zeros((128, 256), np.float32)
    for r in range(128):
        last[r, r // 2] = ROOT_HALF
    wide = np.zeros((128, 256), np.float32)
    wide[:, :128] = pool
    wide[:, 128:] = pool.T
    halves = np.concatenate([wide, stage, fold, spread, unfold, last], axis=0)
    ancestor = np.where(pool.T > 0, 0.0, LOW)
    row_scale = np.where(level_of < 8, 2.0 ** (-level_of / 2.0), 0.0)[:, None] * np.ones((1, 128))
    diag = np.eye(128)
    near = np.full((64, 256), LOW)
    for r in range(64):
        for k in range(192):
            if level_of[64 + r] == 2 + k // 64:
                near[r, k] = 0.0
    far = np.full((16, 256), LOW)
    for r in range(16):
        for k in range(192):
            if level_of[112 + r] == 5 + k // 64:
                far[r, k] = 0.0
    singles = np.concatenate(
        [
            np.concatenate([ancestor, row_scale], axis=1),
            np.concatenate([diag, stage_scale[:, None] * np.ones((1, 128))], axis=1),
            near,
            far,
        ],
        axis=0,
    )
    return halves.astype(np.float32), singles.astype(np.float32)


T_POOL, T_STAGE, T_FOLD, T_SPREAD, T_UNFOLD, T_LAST = 0, 128, 256, 320, 512, 640
T_ROWS = 768
S_ANC, S_DIAG, S_NEAR, S_FAR = 0, 128, 256, 320
S_ROWS = 336
GROUP_AT = (0, 64, 128)
COPIES = 48


def mm(a, b):
    return lax.dot_general(a, b, (((1,), (0,)), ((), ())), preferred_element_type=F32)


def mm_nt(a, b):
    return lax.dot_general(a, b, (((1,), (1,)), ((), ())), preferred_element_type=F32)


def mm_tn(a, b):
    return lax.dot_general(a, b, (((0,), (0,)), ((), ())), preferred_element_type=F32)


def flipped(index, mask):
    for bit in range(8):
        if mask >> bit & 1:
            own = lax.rem(lax.div(index, 1 << bit), 2)
            index = index + (1 << bit) * (1 - 2 * own)
    return index


def kernel(
    heads,
    unroll,
    key_hbm, value_hbm, query_hbm, grad_hbm, half_hbm, single_hbm,
    att_hbm, dquery_hbm, dkey_hbm, dvalue_hbm,
    half_tab, single_tab, rows_in, level_one, coarse_q,
    stage_src, stage_recv,
    local_scores, local_dprob, expo_one, expo_near, expo_far, numer, tops, totals,
    att_buf, dquery_buf, dkv_buf, local_ds, local_probs, adjoint, offset, dcoarse_q, dlocal_kv,
    part_grad, swap_grad, send_grad, recv_grad, one_part, one_send, one_recv, plane_grad, chip_grad,
    load_sem, store_sem, send_sem, recv_sem,
):
    seq = lax.axis_index("seq")
    head = lax.axis_index("head")
    width = heads * DH
    core = lax.rem(seq, 2)
    other = 1 - core
    mate = (seq, 1 - head)
    twin = (flipped(seq, 1), head)
    near_dev = {n: (flipped(seq, n << 1), head) for n, _, _, _ in PARTNERS}
    far_dev = {n: (flipped(seq, n << 4), head) for n, _, _, _ in PARTNERS}
    mine = pl.ds(pl.multiple_of(head * width, width), width)
    theirs = pl.ds(pl.multiple_of((1 - head) * width, width), width)
    sources = (key_hbm, value_hbm, query_hbm, grad_hbm)

    def remote(src, dst, slot, device):
        return pltpu.make_async_remote_copy(
            src_ref=src, dst_ref=dst, send_sem=send_sem.at[slot], recv_sem=recv_sem.at[slot],
            device_id=device, device_id_type=MESH,
        )

    loads = [
        pltpu.make_async_copy(ref.at[:, mine], rows_in.at[i, pl.ds(0, 64)], load_sem.at[i])
        for i, ref in enumerate(sources)
    ]
    table_loads = [
        pltpu.make_async_copy(half_hbm, half_tab, load_sem.at[4]),
        pltpu.make_async_copy(single_hbm, single_tab, load_sem.at[5]),
    ]
    entry = [
        remote(ref.at[:, theirs], rows_in.at[i, pl.ds(64, 64)], i, mate)
        for i, ref in enumerate(sources)
    ]
    own_rows = pl.ds(pl.multiple_of(core * 64, 64), 64)
    twin_rows = pl.ds(pl.multiple_of(other * 64, 64), 64)
    one_swap = [
        remote(level_one.at[kv, own_rows], level_one.at[kv, own_rows], 4 + kv, twin) for kv in (0, 1)
    ]
    one_wait = [
        remote(level_one.at[kv, twin_rows], level_one.at[kv, twin_rows], 4 + kv, twin) for kv in (0, 1)
    ]

    def stage_copies(which, base, devices):
        return {
            n: remote(
                stage_src.at[which, pl.ds(src, count)],
                stage_recv.at[which, core, pl.ds(dst, count)],
                base + n, devices[n],
            )
            for n, src, dst, count in PARTNERS
        }

    def stage_shares(which, base):
        give = [
            remote(
                stage_recv.at[which, core, pl.ds(64 * i, 64)],
                stage_recv.at[which, core, pl.ds(64 * i, 64)], base + i, twin,
            )
            for i in range(3)
        ]
        take = [
            remote(
                stage_recv.at[which, other, pl.ds(64 * i, 64)],
                stage_recv.at[which, other, pl.ds(64 * i, 64)], base + i, twin,
            )
            for i in range(3)
        ]
        return give, take

    near_copies = stage_copies(0, 5, near_dev)
    far_copies = stage_copies(1, 12, far_dev)
    near_give, near_take = stage_shares(0, 20)
    far_give, far_take = stage_shares(1, 23)
    part_swap = [
        remote(part_grad.at[w, other], swap_grad.at[w], 26 + w, twin) for w in (0, 1)
    ]

    def grad_copies(which, base, devices):
        return {
            n: remote(
                send_grad.at[which, pl.ds(dst, count)],
                recv_grad.at[which, pl.ds(dst, count)],
                base + n, devices[n],
            )
            for n, _, dst, count in PARTNERS
        }

    near_back = grad_copies(0, 27, near_dev)
    far_back = grad_copies(1, 34, far_dev)
    one_back_early = remote(one_part.at[other], one_recv.at[other], 42, twin)
    one_take_early = remote(one_part.at[core], one_recv.at[core], 42, twin)
    one_back_late = remote(one_send, one_recv.at[core], 43, twin)
    one_take_late = remote(one_send, one_recv.at[other], 43, twin)
    results = ((att_buf, att_hbm), (dquery_buf, dquery_hbm), (dkv_buf.at[0], dkey_hbm), (dkv_buf.at[1], dvalue_hbm))
    stores = [
        pltpu.make_async_copy(buf.at[pl.ds(0, 64)], out.at[:, mine], store_sem.at[i])
        for i, (buf, out) in enumerate(results)
    ]
    exits = [
        remote(buf.at[pl.ds(64, 64)], out.at[:, mine], 44 + i, mate)
        for i, (buf, out) in enumerate(results)
    ]
    exit_waits = [
        remote(buf.at[pl.ds(64, 64)], out.at[:, theirs], 44 + i, mate)
        for i, (buf, out) in enumerate(results)
    ]

    for copy in loads + table_loads:
        copy.start()
    barrier = pltpu.get_barrier_semaphore()
    partners = [mate, twin] + list(near_dev.values()) + list(far_dev.values())
    for device in partners:
        pl.semaphore_signal(barrier, inc=1, device_id=device, device_id_type=MESH)
    pl.semaphore_wait(barrier, len(partners))
    for copy in entry:
        copy.start()

    def columns(h):
        return pl.ds(pl.multiple_of(h * DH, DH), DH)

    def each_head(*steps):
        def body(i, carry):
            for step in steps:
                for j in range(unroll):
                    step(i * unroll + j)
            return carry

        lax.fori_loop(0, heads // unroll, body, 0)

    for copy in table_loads:
        copy.wait()

    for kv in (0, 1):
        loads[kv].wait()
        entry[kv].wait_recv()

        def pool_one(h):
            cols = columns(h)
            pooled = mm(half_tab[pl.ds(T_POOL, 64), pl.ds(0, 128)], rows_in[kv, :, cols]) * ROOT_HALF
            level_one[kv, own_rows, cols] = pooled.astype(BF16)

        each_head(pool_one)
        one_swap[kv].start()

    loads[2].wait()
    entry[2].wait_recv()

    def pool_queries(h):
        cols = columns(h)
        pooled = mm(half_tab[pl.ds(T_POOL, 128), pl.ds(0, 128)], rows_in[2, :, cols])
        coarse_q[:, cols] = (pooled * single_tab[pl.ds(S_ANC, 128), pl.ds(128, 128)]).astype(BF16)

    each_head(pool_queries)

    for kv in (0, 1):
        one_wait[kv].wait_recv()

    def pool_near(h):
        cols = columns(h)
        pooled = mm(half_tab[pl.ds(T_POOL, 112), pl.ds(0, 128)], level_one[core, :, cols])
        pooled = (pooled * single_tab[pl.ds(S_ANC, 112), pl.ds(128, 128)]).astype(BF16)
        stage_src[0, :, cols] = pooled
        stage_recv[0, core, pl.ds(192, 16), cols] = pooled[96:112]

    each_head(pool_near)
    for copy in near_copies.values():
        copy.start()

    loads[3].wait()
    entry[3].wait_recv()

    def score_local(h):
        cols = columns(h)
        local_scores[h] = mm_nt(rows_in[2, :, cols], rows_in[0, :, cols]) * SCALE
        local_dprob[h] = mm_nt(rows_in[3, :, cols], rows_in[1, :, cols])

    def to_row(column, start, low, count):
        picked = column[low : low + count] * single_tab[pl.ds(S_DIAG + start + low, count), pl.ds(0, 128)]
        return jnp.sum(picked, axis=0, keepdims=True)

    def coarse_forward(h, group, start, rows, low, count, keys, vals, mask, expo):
        cols = columns(h)
        scores = mm_nt(coarse_q[pl.ds(start, rows), cols], keys) * SCALE
        if mask is not None:
            scores = scores + mask
        top = jnp.maximum(jnp.max(scores, axis=1, keepdims=True), FLOOR)
        weights = jnp.exp(scores - top)
        total = jnp.sum(weights, axis=1, keepdims=True)
        expo[h] = weights
        numer[h, pl.ds(GROUP_AT[group], rows)] = mm(weights.astype(BF16), vals)
        tops[h, pl.ds(group, 1)] = to_row(top, start, low, count)
        totals[h, pl.ds(group, 1)] = to_row(total, start, low, count)

    def forward_one(h):
        cols = columns(h)
        coarse_forward(
            h, 0, 0, 64, 0, 64, level_one[0, twin_rows, cols], level_one[1, twin_rows, cols], None, expo_one
        )

    def forward_near(h):
        cols = columns(h)
        coarse_forward(
            h, 1, 64, 64, 0, 56, stage_recv[0, 0, pl.ds(0, 192), cols], stage_recv[0, 1, pl.ds(0, 192), cols],
            single_tab[pl.ds(S_NEAR, 64), pl.ds(0, 192)], expo_near,
        )

    def forward_far(h):
        cols = columns(h)
        coarse_forward(
            h, 2, 112, 16, 8, 8, stage_recv[1, 0, pl.ds(0, 192), cols], stage_recv[1, 1, pl.ds(0, 192), cols],
            single_tab[pl.ds(S_FAR, 16), pl.ds(0, 192)], expo_far,
        )

    each_head(score_local)
    each_head(forward_one)

    for i, group in enumerate(((1,), (2, 3), (4, 5, 6, 7))):
        for n in group:
            near_copies[n].wait_recv()
        near_give[i].start()

    def pool_far(h):
        cols = columns(h)
        pooled = mm(half_tab[pl.ds(T_STAGE, 112), pl.ds(0, 208)], stage_recv[0, core, :, cols])
        pooled = pooled * single_tab[pl.ds(S_DIAG, 112), pl.ds(128, 128)]
        stage_src[1, :, cols] = pooled.astype(BF16)

    each_head(pool_far)
    for copy in far_copies.values():
        copy.start()
    for copy in near_take:
        copy.wait_recv()
    each_head(forward_near)

    for i, group in enumerate(((1,), (2, 3), (4, 5, 6, 7))):
        for n in group:
            far_copies[n].wait_recv()
        far_give[i].start()
    for copy in far_take:
        copy.wait_recv()
    each_head(forward_far)

    def combine(h):
        cols = columns(h)
        top_row = tops[h, pl.ds(0, 1)] + tops[h, pl.ds(1, 1)] + tops[h, pl.ds(2, 1)]
        total_row = totals[h, pl.ds(0, 1)] + totals[h, pl.ds(1, 1)] + totals[h, pl.ds(2, 1)]
        scores = local_scores[h]
        coarse = single_tab[pl.ds(S_ANC, 128), pl.ds(0, 128)] + top_row
        top = jnp.max(jnp.maximum(scores, coarse), axis=1, keepdims=True)
        expo = jnp.exp(scores - top)
        factor = jnp.exp(coarse - top)
        total = jnp.sum(expo + factor * total_row, axis=1, keepdims=True)
        inverse = 1.0 / total
        numer_all = jnp.concatenate(
            [
                numer[h, pl.ds(0, 112)],
                numer[h, pl.ds(112, 16)] + numer[h, pl.ds(128, 16)],
            ],
            axis=0,
        ).astype(BF16)
        outcome = (mm(expo.astype(BF16), rows_in[1, :, cols]) + mm(factor.astype(BF16), numer_all)) * inverse
        att_buf[:, cols] = outcome.astype(BF16)
        grad = rows_in[3, :, cols]
        dots = jnp.sum(grad.astype(F32) * outcome, axis=1, keepdims=True)
        probs = expo * inverse
        weight = (factor * inverse).astype(BF16)
        local_probs[h] = probs.astype(BF16)
        local_ds[h] = (probs * (local_dprob[h] - dots)).astype(BF16)
        adjoint[h] = mm_tn(weight, grad).astype(BF16)
        dots_wide = jnp.broadcast_to(dots, (128, 128))
        dots_high = dots_wide.astype(BF16)
        dots_low = (dots_wide - dots_high.astype(F32)).astype(BF16)
        offset[h] = mm_tn(weight, dots_high) + mm_tn(weight, dots_low)

    each_head(combine)

    def coarse_backward(h, start, rows, keys, vals, expo, dcoarse_at, put_key, put_value):
        cols = columns(h)
        weights = expo[h]
        adj = adjoint[h, pl.ds(start, rows)]
        inner = mm_nt(adj, vals) - offset[h, pl.ds(start, rows), pl.ds(0, 1)]
        dscore = (weights * inner).astype(BF16)
        dcoarse_q[h, pl.ds(dcoarse_at, rows)] = mm(dscore, keys)
        put_key((mm_tn(dscore, coarse_q[pl.ds(start, rows), cols]) * SCALE).astype(BF16))
        put_value(mm_tn(weights.astype(BF16), adj).astype(BF16))

    def backward_far(h):
        cols = columns(h)

        def put_key(x):
            part_grad[1, 0, :, cols] = x

        def put_value(x):
            part_grad[1, 1, :, cols] = x

        coarse_backward(
            h, 112, 16, stage_recv[1, 0, pl.ds(0, 192), cols], stage_recv[1, 1, pl.ds(0, 192), cols],
            expo_far, GROUP_AT[2], put_key, put_value,
        )

    def backward_near(h):
        cols = columns(h)

        def put_key(x):
            part_grad[0, 0, :, cols] = x

        def put_value(x):
            part_grad[0, 1, :, cols] = x

        coarse_backward(
            h, 64, 64, stage_recv[0, 0, pl.ds(0, 192), cols], stage_recv[0, 1, pl.ds(0, 192), cols],
            expo_near, GROUP_AT[1], put_key, put_value,
        )

    def backward_one(h):
        cols = columns(h)

        def put_key(x):
            one_part[0, :, cols] = x

        def put_value(x):
            one_part[1, :, cols] = x

        coarse_backward(
            h, 0, 64, level_one[0, twin_rows, cols], level_one[1, twin_rows, cols],
            expo_one, GROUP_AT[0], put_key, put_value,
        )

    each_head(backward_far)
    part_swap[1].start()
    stores[0].start()
    exits[0].start()
    each_head(backward_one)
    one_back_early.start()

    part_swap[1].wait_recv()

    def sum_far(h):
        cols = columns(h)
        both = part_grad[1, core, :, cols].astype(F32) + swap_grad[1, :, cols].astype(F32)
        send_grad[1, :, cols] = both.astype(BF16)

    each_head(sum_far)
    for copy in far_back.values():
        copy.start()

    each_head(backward_near)
    part_swap[0].start()

    def query_total(h):
        cols = columns(h)
        coarse = jnp.concatenate(
            [
                dcoarse_q[h, pl.ds(0, 112)],
                dcoarse_q[h, pl.ds(112, 16)] + dcoarse_q[h, pl.ds(128, 16)],
            ],
            axis=0,
        ) * single_tab[pl.ds(S_ANC, 128), pl.ds(128, 128)]
        total = mm(local_ds[h], rows_in[0, :, cols])
        total = total + mm(half_tab[pl.ds(T_POOL, 128), pl.ds(128, 128)], coarse.astype(BF16))
        dquery_buf[:, cols] = (total * SCALE).astype(BF16)

    each_head(query_total)
    stores[1].start()
    exits[1].start()

    def local_back(h):
        cols = columns(h)
        dlocal_kv[0, :, cols] = mm_tn(local_ds[h], rows_in[2, :, cols]) * SCALE
        dlocal_kv[1, :, cols] = mm_tn(local_probs[h], rows_in[3, :, cols])

    each_head(local_back)

    for copy in far_back.values():
        copy.wait_recv()
    part_swap[0].wait_recv()

    def sum_near(h):
        cols = columns(h)
        plane = mm(half_tab[pl.ds(T_FOLD, 64), pl.ds(0, 192)], recv_grad[1, :, cols]).astype(BF16)
        plane_grad[:, cols] = plane
        both = part_grad[0, core, :, cols].astype(F32) + swap_grad[0, :, cols].astype(F32)
        both = both + mm(half_tab[pl.ds(T_SPREAD, 192), pl.ds(0, 64)], plane)
        send_grad[0, :, cols] = both.astype(BF16)

    each_head(sum_near)
    for copy in near_back.values():
        copy.start()
    for copy in near_back.values():
        copy.wait_recv()

    def sum_one(h):
        cols = columns(h)
        chip = mm(half_tab[pl.ds(T_UNFOLD, 128), pl.ds(0, 192)], recv_grad[0, :, cols])
        chip = chip + mm(half_tab[pl.ds(T_UNFOLD, 128), pl.ds(192, 64)], plane_grad[:, cols])
        chip_grad[:, cols] = chip

    def sum_one_send(h):
        cols = columns(h)
        one_send[:, cols] = (one_part[core, :, cols].astype(F32) + chip_grad[twin_rows, cols]).astype(BF16)

    each_head(sum_one)
    each_head(sum_one_send)
    one_back_late.start()
    one_take_early.wait_recv()
    one_take_late.wait_recv()

    def finish(h):
        cols = columns(h)
        last = half_tab[pl.ds(T_LAST, 128), pl.ds(0, 64)]
        total = one_recv[core, :, cols].astype(F32) + chip_grad[own_rows, cols]
        dkv_buf[core, :, cols] = (dlocal_kv[core, :, cols] + mm(last, total.astype(BF16))).astype(BF16)
        dkv_buf[other, :, cols] = (dlocal_kv[other, :, cols] + mm(last, one_recv[other, :, cols])).astype(BF16)

    each_head(finish)
    for i in (2, 3):
        stores[i].start()
        exits[i].start()

    for copy in entry + one_swap + near_give + far_give + part_swap + [one_back_early, one_back_late] + exits:
        copy.wait_send()
    for group in (near_copies, far_copies, near_back, far_back):
        for copy in group.values():
            copy.wait_send()
    for copy in stores:
        copy.wait()
    for copy in exit_waits:
        copy.wait_recv()


def solution(mesh):
    halves, singles = tables()
    halves = halves.astype(BF16)
    unroll = 4

    def local(queries, key_rows, values, out_grad):
        rows, columns = queries.shape
        width = columns // 2
        heads = width // DH
        tall = 2 * rows
        anywhere = pl.BlockSpec(memory_space=pl.ANY)
        out = jax.ShapeDtypeStruct((rows, columns), BF16)
        vmem = pltpu.VMEM
        scratch = [
            vmem((T_ROWS, 256), BF16),
            vmem((S_ROWS, 256), F32),
            vmem((4, tall, width), BF16),
            vmem((2, 128, width), BF16),
            vmem((128, width), BF16),
            vmem((2, 112, width), BF16),
            vmem((2, 2, 208, width), BF16),
            vmem((heads, 128, 128), F32),
            vmem((heads, 128, 128), F32),
            vmem((heads, 64, 64), F32),
            vmem((heads, 64, 192), F32),
            vmem((heads, 16, 192), F32),
            vmem((heads, 144, 128), F32),
            vmem((heads, 8, 128), F32),
            vmem((heads, 8, 128), F32),
            vmem((tall, width), BF16),
            vmem((tall, width), BF16),
            vmem((2, tall, width), BF16),
            vmem((heads, 128, 128), BF16),
            vmem((heads, 128, 128), BF16),
            vmem((heads, 128, 128), BF16),
            vmem((heads, 128, 128), F32),
            vmem((heads, 144, 128), F32),
            vmem((2, tall, width), F32),
            vmem((2, 2, 192, width), BF16),
            vmem((2, 192, width), BF16),
            vmem((2, 192, width), BF16),
            vmem((2, 192, width), BF16),
            vmem((2, 64, width), BF16),
            vmem((64, width), BF16),
            vmem((2, 64, width), BF16),
            vmem((64, width), BF16),
            vmem((128, width), F32),
            pltpu.SemaphoreType.DMA((6,)),
            pltpu.SemaphoreType.DMA((4,)),
            pltpu.SemaphoreType.DMA((COPIES,)),
            pltpu.SemaphoreType.DMA((COPIES,)),
        ]
        return pl.pallas_call(
            functools.partial(kernel, heads, unroll),
            out_shape=(out,) * 4,
            in_specs=[anywhere] * 6,
            out_specs=(anywhere,) * 4,
            scratch_shapes=scratch,
            compiler_params=pltpu.CompilerParams(
                collective_id=0, has_side_effects=True, vmem_limit_bytes=60 << 20
            ),
            name="sibling_attention",
        )(key_rows, values, queries, out_grad, jnp.asarray(halves), jnp.asarray(singles))

    spec = P(("seq", "head"), None)
    return jax.shard_map(
        local, mesh=mesh, in_specs=(spec,) * 4, out_specs=(spec,) * 4, check_vma=False
    )
```

time: 1870 us -> 88.1 us (0.05); the launches traced: 1850 us -> 87.9 us
  waiting for transfers between devices: 1240 us -> 0 us
  blocking collectives: 360 us -> 0 us
  local copies, waits for them, and re-layouts: 122 us -> 4.5 us
  Pallas kernels: 0 us -> 82.7 us
  starting transfers between devices: 69.5 us -> 0 us
  other arithmetic: 24.6 us -> 0 us
    unnamed x2 -> x0, waiting for transfers between devices: 1220 us -> none
    all_gather x2 -> x0, blocking collectives: 360 us -> none  [the longest x1 185 us: local(): lax.all_gather(key_pool[level_count], 'seq', axis=0, tiled=True)]
    pallas_call x0 -> x1, Pallas kernels: none -> 82.7 us  [local(): pl.pallas_call(functools.partial(kernel, heads, unroll), out_shape=(out,)...]
    ppermute x24 -> x0, starting transfers between devices: 41 us -> none  [swapped(): return lax.ppermute(block, axis, route)]
    reshape x49 -> x0, local copies, waits for them, and re-layouts: 34.3 us -> none  [the longest x21 13.6 us: local(): jnp.repeat(records[level_no - 1][4], 2 ** level_no, axis=0)]
    all_to_all x8 -> x0, starting transfers between devices: 28.5 us -> none  [the longest x1 4.24 us: local(): lax.all_to_all(query_out, 'head', split_axis=0, concat_axis=1, tiled=True)]
    unnamed x436 -> x10, local copies, waits for them, and re-layouts: 32.2 us -> 4.5 us
  transfers between devices with their start and end apart: 33 -> 0, of which waited for: 13 -> 0; matrix products, arithmetic and copies ran while one was open for 6% -> 0% of each run, Pallas kernels for 0% -> 0%
where the time goes in v1:
time: 88.1 us; the launch traced here: 87.9 us
  Pallas kernels  82.7 us (94%)
  local copies, waits for them, and re-layouts  4.5 us (5%)
    pallas_call x1, Pallas kernels, local(): pl.pallas_call(functools.partial(kernel, heads, unroll), out_shape=(out,)...  82.7 us
    unnamed x10, local copies, waits for them, and re-layouts  4.5 us

profile of v1, /device:TPU:1, one launch (start us, length us, event | category | flops | bytes accessed | tf_op | source)
XLA Modules:
  0.0 87.9 jit_solution(15040877427075285994)
XLA Ops:
  0.6 82.7 %sibling_attention.1 = (bf16[64,2048]{1,0:T(8,128)(2,1)}, bf16[64,2048]{1,0:T(8,128)(2,1)}, bf16[64,2048]{1,0:T(8,128)(2,1)}, bf16[64,2048]{1,0:T(8,128)(2,1)}) custom-call(bf16[64,2048]{1,0:T(8,128)(2,1)} %key_hbm.1, bf16[64,2048]{1,0:T(8,128)(2,1)} %value_hbm.1, bf16[64,2048]{1,0:T(8,128)(2,1)} %query_hbm.1, bf16[64,2048]{1,0:T(8,128)(2,1)} %grad_hbm.1, ...), custom_call_target="tpu_custom_call" | custom-call | tf_op jit(solution)/shard_map/sibling_attention/pallas_call | solution.py:626
  83.3 0.0 copy-start.2
  83.4 1.7 %copy.14 = bf16[64,2048]{1,0:T(8,128)(2,1)} copy(bf16[64,2048]{1,0:T(8,128)(2,1)} %get-tuple-element.8) | data formatting | bytes 524288
  85.1 0.0 copy-done.2
  85.1 0.0 copy-start.1
  85.1 0.7 copy.15
  85.8 0.3 copy-done.1
  86.1 0.0 copy-start
  86.1 0.7 copy.16
  86.8 0.3 copy-done
  87.2 0.7 copy.17
Async XLA Ops:
  83.3 1.7 %copy-start.2 = (bf16[64,2048]{1,0:T(8,128)(2,1)S(1)}, bf16[64,2048]{1,0:T(8,128)(2,1)}, u32[]{:S(2)}) copy-start(bf16[64,2048]{1,0:T(8,128)(2,1)} %get-tuple-element.9) | copy-start | bytes 786436
  85.1 1.0 %copy-start.1 = (bf16[64,2048]{1,0:T(8,128)(2,1)S(1)}, bf16[64,2048]{1,0:T(8,128)(2,1)}, u32[]{:S(2)}) copy-start(bf16[64,2048]{1,0:T(8,128)(2,1)} %get-tuple-element.10) | copy-start | bytes 786436
  86.1 1.0 %copy-start = (bf16[64,2048]{1,0:T(8,128)(2,1)S(1)}, bf16[64,2048]{1,0:T(8,128)(2,1)}, u32[]{:S(2)}) copy-start(bf16[64,2048]{1,0:T(8,128)(2,1)} %get-tuple-element.11) | copy-start | bytes 786436

commit v2 on v1

v2 whole, which is shorter than its diff:
```python
import functools
import math

import jax
import jax.numpy as jnp
import numpy as np
from jax import lax
from jax.experimental import pallas as pl
from jax.experimental.pallas import tpu as pltpu
from jax.sharding import PartitionSpec as P

MESH = pl.DeviceIdType.MESH
BF16 = jnp.bfloat16
F32 = jnp.float32
DH = 128
SCALE = 1.0 / math.sqrt(DH)
LOW = -1e30
FLOOR = -1e29

NEAR = ((1, 64, 0, 32), (2, 96, 32, 16), (3, 96, 48, 16))
FAR = ((1, 0, 0, 64), (2, 64, 64, 32), (3, 64, 96, 32))
FAR += tuple((n, 96, 128 + 16 * (n - 4), 16) for n in (4, 5, 6, 7))
PLANE = 16


def tables():
    level_of = np.zeros(128, np.int64)
    pool = np.zeros((128, 128), np.float32)
    row = 0
    for level in range(1, 8):
        for i in range(128 >> level):
            pool[row, i << level : (i + 1) << level] = 1.0
            level_of[row] = level
            row += 1
    level_of[127] = 99
    wide = np.concatenate([pool, pool.T], axis=1)
    pick = np.zeros((2, 128, 256), np.float32)
    compact = np.zeros((2, 128, 256), np.float32)
    fold = np.zeros((128, 256), np.float32)
    for kv in range(2):
        for i in range(PLANE):
            for r in range(8):
                pick[kv, 8 * i + r, 16 * i + 8 * kv + r] = 1.0
            for r in range(4):
                compact[kv, 4 * i + r, 16 * i + 8 * kv + r] = 1.0
            for r in range(2):
                compact[kv, 64 + 2 * i + r, 16 * i + 8 * kv + 4 + r] = 1.0
            compact[kv, 96 + i, 16 * i + 8 * kv + 6] = 1.0
    for i in range(PLANE):
        for r in range(4):
            fold[8 * i + r, 4 * i + r] = 1.0
        for r in range(2):
            for j in range(2):
                fold[8 * i + 4 + r, 64 + 32 * j + 2 * i + r] = 1.0
        for j in range(4):
            fold[8 * i + 6, 128 + 16 * j + i] = 1.0
    halves = np.concatenate([wide, pick[0], pick[1], compact[0], compact[1], fold], axis=0)
    ancestor = np.where(pool.T > 0, 0.0, LOW)
    row_scale = np.where(level_of < 8, 2.0 ** (-level_of / 2.0), 0.0)[:, None] * np.ones((1, 128))
    shard = np.arange(128) // 8
    across = np.where(shard[:, None] // 8 != shard[None, :] // 8, 0.0, LOW)
    near = np.full((48, 256), LOW)
    for r in range(48):
        for k in range(128):
            if level_of[64 + r] == (2 if k % 64 < 32 else 3):
                near[r, k] = 0.0
    far = np.full((128, 256), LOW)
    for r in range(128):
        for k in range(192):
            if level_of[120 + r % 8] == 5 + k // 64:
                far[r, k] = 0.0
    singles = np.concatenate(
        [
            np.concatenate([ancestor, row_scale], axis=1),
            np.concatenate([np.eye(128), across], axis=1),
            near,
            far,
        ],
        axis=0,
    )
    return halves.astype(np.float32), singles.astype(np.float32)


T_POOL, T_PICK, T_COMPACT, T_FOLD = 0, 128, 384, 640
T_ROWS = 768
S_ANC, S_DIAG, S_NEAR, S_FAR = 0, 128, 256, 304
S_ROWS = 432

C_ENTRY, C_EXIT, C_ONE, C_SHARE, C_PART, C_ONE_BACK = 0, 4, 8, 9, 10, 11
C_NEAR, C_NEAR_BACK, C_FAR, C_FAR_BACK = 11, 14, 17, 24
C_ROWS, C_QUERY, C_SUMS, C_ADJ, C_DQUERY, C_DROWS = 32, 48, 64, 80, 96, 112
COPIES = 128


def mm(a, b):
    return lax.dot_general(a, b, (((1,), (0,)), ((), ())), preferred_element_type=F32)


def mm_nt(a, b):
    return lax.dot_general(a, b, (((1,), (1,)), ((), ())), preferred_element_type=F32)


def mm_tn(a, b):
    return lax.dot_general(a, b, (((0,), (0,)), ((), ())), preferred_element_type=F32)


def flipped(index, mask):
    for bit in range(8):
        if mask >> bit & 1:
            own = lax.rem(lax.div(index, 1 << bit), 2)
            index = index + (1 << bit) * (1 - 2 * own)
    return index


def kernel(
    heads,
    unroll,
    key_hbm, value_hbm, query_hbm, grad_hbm, half_hbm, single_hbm,
    att_hbm, dquery_hbm, dkey_hbm, dvalue_hbm,
    half_tab, single_tab, rows_in, coarse_kv, coarse_q, one_kv, near_kv,
    rows_send, rows_recv, query_send, query_recv, far_send, far_kv, pair_kv,
    local_scores, local_dprob, expo_one, expo_near, expo_far, numer, tops, totals,
    sums_send, sums_recv, adj_send, adj_recv, dquery_send, dquery_recv, drows_send, drows_recv,
    dfar_send, dfar_recv,
    att_buf, dquery_buf, dkv_buf, local_ds, local_probs, adjoint, offset, dcoarse_q, dlocal_kv,
    part_grad, swap_grad, send_grad, recv_grad, one_part, one_recv,
    load_sem, store_sem, self_sem, send_sem, recv_sem,
):
    seq = lax.axis_index("seq")
    head = lax.axis_index("head")
    width = heads * DH
    core = lax.rem(seq, 2)
    place = lax.rem(seq, PLANE)
    chip = lax.div(place, 2)
    mate = (seq, 1 - head)
    twin = (flipped(seq, 1), head)
    near_dev = {n: (flipped(seq, n << 1), head) for n, _, _, _ in NEAR}
    far_dev = {n: (flipped(seq, n << 4), head) for n, _, _, _ in FAR}
    peers = []
    for m in range(PLANE):
        there = flipped(seq, m)
        slot = lax.rem(there, PLANE)
        peers.append(((there, head), slot, lax.div(slot, 2), lax.rem(slot, 2)))
    mine = pl.ds(pl.multiple_of(head * width, width), width)
    theirs = pl.ds(pl.multiple_of((1 - head) * width, width), width)
    sources = (key_hbm, value_hbm, query_hbm, grad_hbm)

    def remote(src, dst, slot, device):
        return pltpu.make_async_remote_copy(
            src_ref=src, dst_ref=dst, send_sem=send_sem.at[slot], recv_sem=recv_sem.at[slot],
            device_id=device, device_id_type=MESH,
        )

    def slab(slot, rows):
        return pl.ds(pl.multiple_of(slot * rows, rows), rows)

    loads = [
        pltpu.make_async_copy(ref.at[:, mine], rows_in.at[i, pl.ds(0, 64)], load_sem.at[i])
        for i, ref in enumerate(sources)
    ]
    table_loads = [
        pltpu.make_async_copy(half_hbm, half_tab, load_sem.at[4]),
        pltpu.make_async_copy(single_hbm, single_tab, load_sem.at[5]),
    ]
    entry = [
        remote(ref.at[:, theirs], rows_in.at[i, pl.ds(64, 64)], C_ENTRY + i, mate)
        for i, ref in enumerate(sources)
    ]
    one_swap = remote(coarse_kv.at[:, pl.ds(0, 64)], one_kv, C_ONE, twin)
    near_copies = [
        remote(coarse_kv.at[:, pl.ds(src, count)], near_kv.at[0, :, pl.ds(dst, count)], C_NEAR + n, near_dev[n])
        for n, src, dst, count in NEAR
    ]
    share = remote(near_kv.at[0], near_kv.at[1], C_SHARE, twin)
    far_copies = [
        remote(far_send.at[pl.ds(src, count)], far_kv.at[pl.ds(dst, count)], C_FAR + n, far_dev[n])
        for n, src, dst, count in FAR
    ]
    far_back = [
        remote(dfar_send.at[pl.ds(dst, count)], dfar_recv.at[pl.ds(dst, count)], C_FAR_BACK + n, far_dev[n])
        for n, _, dst, count in FAR
    ]
    part_swap = remote(part_grad.at[1], swap_grad, C_PART, twin)
    near_back = [
        remote(send_grad.at[:, pl.ds(dst, count)], recv_grad.at[:, pl.ds(dst, count)], C_NEAR_BACK + n, near_dev[n])
        for n, _, dst, count in NEAR
    ]
    one_back = remote(one_part, one_recv, C_ONE_BACK, twin)

    class Spread:
        def __init__(self, which, base, send, recv, rows):
            self.local = pltpu.make_async_copy(
                send.at[chip, core], recv.at[slab(place, rows)], self_sem.at[which]
            )
            self.out = []
            self.come = []
            for m in range(1, PLANE):
                device, slot, owner, group = peers[m]
                self.out.append(remote(send.at[owner, group], recv.at[slab(place, rows)], base + m, device))
                self.come.append(remote(send.at[owner, group], recv.at[slab(slot, rows)], base + m, device))

        def start(self):
            for copy in self.out:
                copy.start()
            self.local.start()

        def wait_recv(self):
            self.local.wait()
            for copy in self.come:
                copy.wait_recv()

        def wait_send(self):
            for copy in self.out:
                copy.wait_send()

    class Return(Spread):
        def __init__(self, which, base, send, recv, rows):
            self.local = pltpu.make_async_copy(
                send.at[slab(place, rows)], recv.at[chip, core], self_sem.at[which]
            )
            self.out = []
            self.come = []
            for m in range(1, PLANE):
                device, slot, owner, group = peers[m]
                self.out.append(remote(send.at[slab(slot, rows)], recv.at[chip, core], base + m, device))
                self.come.append(remote(send.at[slab(slot, rows)], recv.at[owner, group], base + m, device))

    rows_out = Spread(0, C_ROWS, rows_send, rows_recv, 16)
    query_out = Spread(1, C_QUERY, query_send, query_recv, 8)
    sums_back = Return(2, C_SUMS, sums_send, sums_recv, 16)
    adj_out = Spread(3, C_ADJ, adj_send, adj_recv, 16)
    dquery_back = Return(4, C_DQUERY, dquery_send, dquery_recv, 8)
    drows_back = Return(5, C_DROWS, drows_send, drows_recv, 16)

    results = ((att_buf, att_hbm), (dquery_buf, dquery_hbm), (dkv_buf.at[0], dkey_hbm), (dkv_buf.at[1], dvalue_hbm))
    stores = [
        pltpu.make_async_copy(buf.at[pl.ds(0, 64)], out.at[:, mine], store_sem.at[i])
        for i, (buf, out) in enumerate(results)
    ]
    exits = [
        remote(buf.at[pl.ds(64, 64)], out.at[:, mine], C_EXIT + i, mate)
        for i, (buf, out) in enumerate(results)
    ]
    exit_waits = [
        remote(buf.at[pl.ds(64, 64)], out.at[:, theirs], C_EXIT + i, mate)
        for i, (buf, out) in enumerate(results)
    ]

    for copy in loads + table_loads:
        copy.start()
    barrier = pltpu.get_barrier_semaphore()
    partners = [mate] + [peer[0] for peer in peers[1:]] + list(far_dev.values())
    for device in partners:
        pl.semaphore_signal(barrier, inc=1, device_id=device, device_id_type=MESH)
    pl.semaphore_wait(barrier, len(partners))
    for copy in entry:
        copy.start()

    def columns(h):
        return pl.ds(pl.multiple_of(h * DH, DH), DH)

    def each_head(*steps):
        def body(i, carry):
            for step in steps:
                for j in range(unroll):
                    step(i * unroll + j)
            return carry

        lax.fori_loop(0, heads // unroll, body, 0)

    for copy in table_loads:
        copy.wait()
    everything = pl.ds(0, 128)
    right = pl.ds(128, 128)

    def pooled(which, h):
        rows = mm(half_tab[pl.ds(T_POOL, 128), pl.ds(0, 128)], rows_in[which, :, columns(h)])
        return rows * single_tab[pl.ds(S_ANC, 128), right]

    for kv in (0, 1):
        loads[kv].wait()
        entry[kv].wait_recv()

    def pool_rows(h):
        cols = columns(h)
        keys = pooled(0, h)
        vals = pooled(1, h)
        coarse_kv[0, :, cols] = keys.astype(BF16)
        coarse_kv[1, :, cols] = vals.astype(BF16)
        for group in (0, 1):
            low = 112 + 8 * group
            both = jnp.concatenate([keys[low : low + 8], vals[low : low + 8]], axis=0)
            rows_send[h, group] = both.astype(BF16)

    each_head(pool_rows)
    rows_out.start()
    for copy in near_copies:
        copy.start()
    one_swap.start()

    loads[2].wait()
    entry[2].wait_recv()

    def pool_queries(h):
        rows = pooled(2, h)
        short = rows.astype(BF16)
        coarse_q[:, columns(h)] = short
        for group in (0, 1):
            query_send[h, group] = short.astype(F32)[112 + 8 * group : 120 + 8 * group]

    each_head(pool_queries)
    query_out.start()

    rows_out.wait_recv()

    @pl.when(core == 1)
    def _():
        for kv in (0, 1):
            rows = mm(half_tab[pl.ds(T_COMPACT + 128 * kv, 112)], rows_recv[...])
            far_send[:, pl.ds(128 * kv, 128)] = rows.astype(BF16)
        for copy in far_copies:
            copy.start()

    @pl.when(core == 0)
    def _():
        for kv in (0, 1):
            rows = mm(half_tab[pl.ds(T_PICK + 128 * kv, 128)], rows_recv[...])
            pair_kv[:, pl.ds(128 * kv, 128)] = rows.astype(BF16)

    def to_row(column, start):
        count = column.shape[0]
        picked = column * single_tab[pl.ds(S_DIAG + start, count), everything]
        return jnp.sum(picked, axis=0, keepdims=True)

    def attend(queries, keys, vals, mask):
        scores = mm_nt(queries, keys) * SCALE
        if mask is not None:
            scores = scores + mask
        top = jnp.maximum(jnp.max(scores, axis=1, keepdims=True), FLOOR)
        weights = jnp.exp(scores - top)
        total = jnp.sum(weights, axis=1, keepdims=True)
        return weights, top, total, mm(weights.astype(BF16), vals)

    def attend_back(weights, adj, shift, queries, keys, vals):
        inner = mm_nt(adj, vals) - shift
        dscore = (weights * inner).astype(BF16)
        dkeys = mm_tn(dscore, queries) * SCALE
        return mm(dscore, keys), dkeys, mm_tn(weights.astype(BF16), adj)

    def near_rows(kv, h):
        return jnp.concatenate([near_kv[0, kv, :, columns(h)], near_kv[1, kv, :, columns(h)]], axis=0)

    def forward_one(h):
        cols = columns(h)
        weights, top, total, sums = attend(
            coarse_q[pl.ds(0, 64), cols], one_kv[0, :, cols], one_kv[1, :, cols], None
        )
        expo_one[h] = weights
        numer[h, pl.ds(0, 64)] = sums
        tops[h, pl.ds(0, 1)] = to_row(top, 0)
        totals[h, pl.ds(0, 1)] = to_row(total, 0)

    def forward_near(h):
        weights, top, total, sums = attend(
            coarse_q[pl.ds(64, 48), columns(h)], near_rows(0, h), near_rows(1, h),
            single_tab[pl.ds(S_NEAR, 48), everything],
        )
        expo_near[h] = weights
        numer[h, pl.ds(64, 48)] = sums
        tops[h, pl.ds(1, 1)] = to_row(top, 64)
        totals[h, pl.ds(1, 1)] = to_row(total, 64)

    one_swap.wait_recv()
    each_head(forward_one)
    for copy in near_copies:
        copy.wait_recv()
    share.start()

    query_out.wait_recv()

    def forward_far(keys, vals, mask, span):
        weights, top, total, sums = attend(query_recv[...].astype(BF16), keys, vals, mask)
        expo_far[:, pl.ds(0, span)] = weights
        lanes = lax.broadcasted_iota(jnp.int32, (128, 128), 1)
        pair = jnp.where(lanes < 64, top, total)
        whole = jnp.concatenate([sums.reshape(PLANE, 8, 128), pair.reshape(PLANE, 8, 128)], axis=1)
        sums_send[...] = whole.reshape(PLANE * 16, 128)

    @pl.when(core == 0)
    def _():
        forward_far(
            pair_kv[:, everything], pair_kv[:, right], single_tab[pl.ds(S_DIAG, 128), right], 128
        )

    @pl.when(core == 1)
    def _():
        for copy in far_copies:
            copy.wait_recv()
        forward_far(
            far_kv[:, everything], far_kv[:, right], single_tab[pl.ds(S_FAR, 128), pl.ds(0, 192)], 192
        )

    sums_back.start()

    loads[3].wait()
    entry[3].wait_recv()

    def score_local(h):
        cols = columns(h)
        local_scores[h] = mm_nt(rows_in[2, :, cols], rows_in[0, :, cols]) * SCALE
        local_dprob[h] = mm_nt(rows_in[3, :, cols], rows_in[1, :, cols])

    each_head(score_local)
    share.wait_recv()
    each_head(forward_near)
    sums_back.wait_recv()

    def combine(h):
        cols = columns(h)
        top_row = tops[h, pl.ds(0, 1)] + tops[h, pl.ds(1, 1)]
        total_row = totals[h, pl.ds(0, 1)] + totals[h, pl.ds(1, 1)]
        for group in (0, 1):
            top_row = top_row + to_row(sums_recv[h, group, pl.ds(8, 8), pl.ds(0, 1)], 112 + 8 * group)
            total_row = total_row + to_row(sums_recv[h, group, pl.ds(8, 8), pl.ds(64, 1)], 112 + 8 * group)
        scores = local_scores[h]
        coarse = single_tab[pl.ds(S_ANC, 128), everything] + top_row
        top = jnp.max(jnp.maximum(scores, coarse), axis=1, keepdims=True)
        expo = jnp.exp(scores - top)
        factor = jnp.exp(coarse - top)
        total = jnp.sum(expo + factor * total_row, axis=1, keepdims=True)
        inverse = 1.0 / total
        numer_all = jnp.concatenate(
            [numer[h], sums_recv[h, 0, pl.ds(0, 8)], sums_recv[h, 1, pl.ds(0, 8)]], axis=0
        ).astype(BF16)
        outcome = (mm(expo.astype(BF16), rows_in[1, :, cols]) + mm(factor.astype(BF16), numer_all)) * inverse
        att_buf[:, cols] = outcome.astype(BF16)
        grad = rows_in[3, :, cols]
        dots = jnp.sum(grad.astype(F32) * outcome, axis=1, keepdims=True)
        probs = expo * inverse
        weight = (factor * inverse).astype(BF16)
        local_probs[h] = probs.astype(BF16)
        local_ds[h] = (probs * (local_dprob[h] - dots)).astype(BF16)
        adj = mm_tn(weight, grad)
        adjoint[h] = adj.astype(BF16)
        dots_wide = jnp.broadcast_to(dots, (128, 128))
        dots_high = dots_wide.astype(BF16)
        dots_low = (dots_wide - dots_high.astype(F32)).astype(BF16)
        shift = mm_tn(weight, dots_high) + mm_tn(weight, dots_low)
        offset[h] = shift
        for group in (0, 1):
            low = 112 + 8 * group
            adj_send[h, group, pl.ds(0, 8)] = adj[low : low + 8]
            adj_send[h, group, pl.ds(8, 8)] = shift[low : low + 8]

    each_head(combine)
    adj_out.start()
    stores[0].start()
    exits[0].start()

    def backward_near(h):
        cols = columns(h)
        dqueries, dkeys, dvals = attend_back(
            expo_near[h], adjoint[h, pl.ds(64, 48)], offset[h, pl.ds(64, 48), pl.ds(0, 1)],
            coarse_q[pl.ds(64, 48), cols], near_rows(0, h), near_rows(1, h),
        )
        dcoarse_q[h, pl.ds(64, 48)] = dqueries
        for side in (0, 1):
            part_grad[side, 0, :, cols] = dkeys[64 * side : 64 * side + 64].astype(BF16)
            part_grad[side, 1, :, cols] = dvals[64 * side : 64 * side + 64].astype(BF16)

    def backward_one(h):
        cols = columns(h)
        dqueries, dkeys, dvals = attend_back(
            expo_one[h], adjoint[h, pl.ds(0, 64)], offset[h, pl.ds(0, 64), pl.ds(0, 1)],
            coarse_q[pl.ds(0, 64), cols], one_kv[0, :, cols], one_kv[1, :, cols],
        )
        dcoarse_q[h, pl.ds(0, 64)] = dqueries
        one_part[0, :, cols] = dkeys.astype(BF16)
        one_part[1, :, cols] = dvals.astype(BF16)

    each_head(backward_near)
    part_swap.start()
    adj_out.wait_recv()

    def backward_far(keys, vals, span):
        arrived = adj_recv[...].reshape(PLANE, 16, 128)
        adj = arrived[:, 0:8].reshape(128, 128).astype(BF16)
        shift = arrived[:, 8:16].reshape(128, 128)[:, 0:1]
        return attend_back(
            expo_far[:, pl.ds(0, span)], adj, shift, query_recv[...].astype(BF16), keys, vals
        )

    def put_rows(dkeys, dvals):
        whole = jnp.concatenate([dkeys.reshape(PLANE, 8, 128), dvals.reshape(PLANE, 8, 128)], axis=1)
        drows_send[...] = whole.reshape(PLANE * 16, 128)

    @pl.when(core == 0)
    def _():
        dqueries, dkeys, dvals = backward_far(pair_kv[:, everything], pair_kv[:, right], 128)
        dquery_send[...] = dqueries
        put_rows(dkeys, dvals)

    @pl.when(core == 1)
    def _():
        dqueries, dkeys, dvals = backward_far(far_kv[:, everything], far_kv[:, right], 192)
        dquery_send[...] = dqueries
        dfar_send[:, everything] = dkeys.astype(BF16)
        dfar_send[:, right] = dvals.astype(BF16)
        for copy in far_back:
            copy.start()

    dquery_back.start()

    @pl.when(core == 0)
    def _():
        for copy in drows_back.out:
            copy.start()
        drows_back.local.start()

    part_swap.wait_recv()

    def sum_near(h):
        cols = columns(h)
        for kv in (0, 1):
            both = part_grad[0, kv, :, cols].astype(F32) + swap_grad[kv, :, cols].astype(F32)
            send_grad[kv, :, cols] = both.astype(BF16)

    each_head(sum_near)
    for copy in near_back:
        copy.start()
    each_head(backward_one)
    one_back.start()

    @pl.when(core == 1)
    def _():
        for copy in far_back:
            copy.wait_recv()
        both = mm(half_tab[pl.ds(T_FOLD, 128), pl.ds(0, 192)], dfar_recv[...])
        put_rows(both[:, 0:128], both[:, 128:256])
        for copy in drows_back.out:
            copy.start()
        drows_back.local.start()

    dquery_back.wait_recv()

    def unpooled(rows):
        scaled = rows * single_tab[pl.ds(S_ANC, 128), right]
        return mm(half_tab[pl.ds(T_POOL, 128), right], scaled.astype(BF16))

    def query_total(h):
        cols = columns(h)
        coarse = jnp.concatenate([dcoarse_q[h], dquery_recv[h, 0], dquery_recv[h, 1]], axis=0)
        total = mm(local_ds[h], rows_in[0, :, cols]) + unpooled(coarse)
        dquery_buf[:, cols] = (total * SCALE).astype(BF16)

    each_head(query_total)
    stores[1].start()
    exits[1].start()

    def local_back(h):
        cols = columns(h)
        dlocal_kv[0, :, cols] = mm_tn(local_ds[h], rows_in[2, :, cols]) * SCALE
        dlocal_kv[1, :, cols] = mm_tn(local_probs[h], rows_in[3, :, cols])

    each_head(local_back)
    one_back.wait_recv()
    for copy in near_back:
        copy.wait_recv()
    drows_back.wait_recv()

    def finish(kv):
        def step(h):
            cols = columns(h)
            coarse = jnp.concatenate(
                [
                    one_recv[kv, :, cols].astype(F32),
                    recv_grad[kv, pl.ds(0, 32), cols].astype(F32),
                    recv_grad[kv, pl.ds(32, 16), cols].astype(F32)
                    + recv_grad[kv, pl.ds(48, 16), cols].astype(F32),
                    drows_recv[h, 0, pl.ds(8 * kv, 8)],
                    drows_recv[h, 1, pl.ds(8 * kv, 8)],
                ],
                axis=0,
            )
            dkv_buf[kv, :, cols] = (dlocal_kv[kv, :, cols] + unpooled(coarse)).astype(BF16)

        return step

    for kv in (0, 1):
        each_head(finish(kv))
        stores[2 + kv].start()
        exits[2 + kv].start()

    for copy in entry + near_copies + near_back + [one_swap, share, part_swap, one_back] + exits:
        copy.wait_send()
    for copy in (rows_out, query_out, sums_back, adj_out, dquery_back, drows_back):
        copy.wait_send()

    @pl.when(core == 1)
    def _():
        for copy in far_copies + far_back:
            copy.wait_send()

    for copy in stores:
        copy.wait()
    for copy in exit_waits:
        copy.wait_recv()


def solution(mesh):
    halves, singles = tables()
    halves = halves.astype(BF16)
    unroll = 4

    def local(queries, key_rows, values, out_grad):
        rows, columns = queries.shape
        width = columns // 2
        heads = width // DH
        tall = 2 * rows
        anywhere = pl.BlockSpec(memory_space=pl.ANY)
        out = jax.ShapeDtypeStruct((rows, columns), BF16)
        vmem = pltpu.VMEM
        scratch = [
            vmem((T_ROWS, 256), BF16),
            vmem((S_ROWS, 256), F32),
            vmem((4, tall, width), BF16),
            vmem((2, 128, width), BF16),
            vmem((128, width), BF16),
            vmem((2, 64, width), BF16),
            vmem((2, 2, 64, width), BF16),
            vmem((heads, 2, 16, 128), BF16),
            vmem((PLANE * 16, 128), BF16),
            vmem((heads, 2, 8, 128), F32),
            vmem((PLANE * 8, 128), F32),
            vmem((112, 256), BF16),
            vmem((192, 256), BF16),
            vmem((128, 256), BF16),
            vmem((heads, 128, 128), F32),
            vmem((heads, 128, 128), F32),
            vmem((heads, 64, 64), F32),
            vmem((heads, 48, 128), F32),
            vmem((128, 192), F32),
            vmem((heads, 112, 128), F32),
            vmem((heads, 8, 128), F32),
            vmem((heads, 8, 128), F32),
            vmem((PLANE * 16, 128), F32),
            vmem((heads, 2, 16, 128), F32),
            vmem((heads, 2, 16, 128), F32),
            vmem((PLANE * 16, 128), F32),
            vmem((PLANE * 8, 128), F32),
            vmem((heads, 2, 8, 128), F32),
            vmem((PLANE * 16, 128), F32),
            vmem((heads, 2, 16, 128), F32),
            vmem((192, 256), BF16),
            vmem((192, 256), BF16),
            vmem((tall, width), BF16),
            vmem((tall, width), BF16),
            vmem((2, tall, width), BF16),
            vmem((heads, 128, 128), BF16),
            vmem((heads, 128, 128), BF16),
            vmem((heads, 128, 128), BF16),
            vmem((heads, 128, 128), F32),
            vmem((heads, 112, 128), F32),
            vmem((2, tall, width), F32),
            vmem((2, 2, 64, width), BF16),
            vmem((2, 64, width), BF16),
            vmem((2, 64, width), BF16),
            vmem((2, 64, width), BF16),
            vmem((2, 64, width), BF16),
            vmem((2, 64, width), BF16),
            pltpu.SemaphoreType.DMA((6,)),
            pltpu.SemaphoreType.DMA((4,)),
            pltpu.SemaphoreType.DMA((6,)),
            pltpu.SemaphoreType.DMA((COPIES,)),
            pltpu.SemaphoreType.DMA((COPIES,)),
        ]
        return pl.pallas_call(
            functools.partial(kernel, heads, unroll),
            out_shape=(out,) * 4,
            in_specs=[anywhere] * 6,
            out_specs=(anywhere,) * 4,
            scratch_shapes=scratch,
            compiler_params=pltpu.CompilerParams(
                collective_id=0, has_side_effects=True, vmem_limit_bytes=60 << 20
            ),
            name="sibling_attention",
        )(key_rows, values, queries, out_grad, jnp.asarray(halves), jnp.asarray(singles))

    spec = P(("seq", "head"), None)
    return jax.shard_map(
        local, mesh=mesh, in_specs=(spec,) * 4, out_specs=(spec,) * 4, check_vma=False
    )
```

time: 88.1 us -> 66.8 us (0.76)
  Pallas kernels: 82.7 us -> 61.5 us
    pallas_call x1, Pallas kernels: 82.7 us -> 61.5 us  [local(): pl.pallas_call(functools.partial(kernel, heads, unroll), out_shape=(out,)...]
where the time goes in v2:
time: 66.8 us; the launch traced here: 66.7 us
  Pallas kernels  61.5 us (92%)
  local copies, waits for them, and re-layouts  4.5 us (7%)
    pallas_call x1, Pallas kernels, local(): pl.pallas_call(functools.partial(kernel, heads, unroll), out_shape=(out,)...  61.5 us
    unnamed x10, local copies, waits for them, and re-layouts  4.5 us

profile of v2, /device:TPU:1, one launch (start us, length us, event | category | flops | bytes accessed | tf_op | source)
XLA Modules:
  0.0 66.7 jit_solution(1465039092883294165)
XLA Ops:
  0.6 61.5 %sibling_attention.1 = (bf16[64,2048]{1,0:T(8,128)(2,1)}, bf16[64,2048]{1,0:T(8,128)(2,1)}, bf16[64,2048]{1,0:T(8,128)(2,1)}, bf16[64,2048]{1,0:T(8,128)(2,1)}) custom-call(bf16[64,2048]{1,0:T(8,128)(2,1)} %key_hbm.1, bf16[64,2048]{1,0:T(8,128)(2,1)} %value_hbm.1, bf16[64,2048]{1,0:T(8,128)(2,1)} %query_hbm.1, bf16[64,2048]{1,0:T(8,128)(2,1)} %grad_hbm.1, ...), custom_call_target="tpu_custom_call" | custom-call | tf_op jit(solution)/shard_map/sibling_attention/pallas_call | solution.py:677
  62.1 0.0 copy-start.2
  62.2 1.7 %copy.14 = bf16[64,2048]{1,0:T(8,128)(2,1)} copy(bf16[64,2048]{1,0:T(8,128)(2,1)} %get-tuple-element.8) | data formatting | bytes 524288
  63.9 0.0 copy-done.2
  63.9 0.0 copy-start.1
  63.9 0.7 %copy.15 = bf16[64,2048]{1,0:T(8,128)(2,1)} copy(bf16[64,2048]{1,0:T(8,128)(2,1)S(1)} %copy-done.2) | data formatting | bytes 524288
  64.6 0.3 copy-done.1
  64.9 0.0 copy-start
  64.9 0.7 %copy.16 = bf16[64,2048]{1,0:T(8,128)(2,1)} copy(bf16[64,2048]{1,0:T(8,128)(2,1)S(1)} %copy-done.1) | data formatting | bytes 524288
  65.6 0.3 copy-done
  66.0 0.7 %copy.17 = bf16[64,2048]{1,0:T(8,128)(2,1)} copy(bf16[64,2048]{1,0:T(8,128)(2,1)S(1)} %copy-done) | data formatting | bytes 524288
Async XLA Ops:
  62.1 1.7 %copy-start.2 = (bf16[64,2048]{1,0:T(8,128)(2,1)S(1)}, bf16[64,2048]{1,0:T(8,128)(2,1)}, u32[]{:S(2)}) copy-start(bf16[64,2048]{1,0:T(8,128)(2,1)} %get-tuple-element.9) | copy-start | bytes 786436
  63.9 1.0 %copy-start.1 = (bf16[64,2048]{1,0:T(8,128)(2,1)S(1)}, bf16[64,2048]{1,0:T(8,128)(2,1)}, u32[]{:S(2)}) copy-start(bf16[64,2048]{1,0:T(8,128)(2,1)} %get-tuple-element.10) | copy-start | bytes 786436
  64.9 1.0 %copy-start = (bf16[64,2048]{1,0:T(8,128)(2,1)S(1)}, bf16[64,2048]{1,0:T(8,128)(2,1)}, u32[]{:S(2)}) copy-start(bf16[64,2048]{1,0:T(8,128)(2,1)} %get-tuple-element.11) | copy-start | bytes 786436

commit v3 on v2

--- a/solution.py
+++ b/solution.py
@@ -33,30 +33,42 @@
             level_of[row] = level
             row += 1
     level_of[127] = 99
-    wide = np.concatenate([pool, pool.T], axis=1)
-    pick = np.zeros((2, 128, 256), np.float32)
-    compact = np.zeros((2, 128, 256), np.float32)
-    fold = np.zeros((128, 256), np.float32)
-    for kv in range(2):
-        for i in range(PLANE):
-            for r in range(8):
-                pick[kv, 8 * i + r, 16 * i + 8 * kv + r] = 1.0
-            for r in range(4):
-                compact[kv, 4 * i + r, 16 * i + 8 * kv + r] = 1.0
+    pick = np.zeros((3, 128, 512), np.float32)
+    pick_far = np.zeros((128, 512), np.float32)
+    compact = np.zeros((2, 128, 512), np.float32)
+    for i in range(PLANE):
+        for half in range(2):
+            at = 32 * i + 16 * half
+            for x in range(3):
+                for r in range(4):
+                    pick[x, 8 * i + 4 * half + r, at + 4 * x + r] = 1.0
             for r in range(2):
-                compact[kv, 64 + 2 * i + r, 16 * i + 8 * kv + 4 + r] = 1.0
-            compact[kv, 96 + i, 16 * i + 8 * kv + 6] = 1.0
-    for i in range(PLANE):
+                pick_far[8 * i + 2 * half + r, at + 8 + r] = 1.0
+            pick_far[8 * i + 4 + half, at + 10] = 1.0
+            pick_far[8 * i + 6, at + 11] = 1.0
+            for kv in range(2):
+                for r in range(2):
+                    compact[kv, 4 * i + 2 * half + r, at + 4 * kv + r] = 1.0
+                compact[kv, 64 + 2 * i + half, at + 4 * kv + 2] = 1.0
+                compact[kv, 96 + i, at + 4 * kv + 3] = 1.0
+    blocks = [pick[0], pick[1], pick[2], pick_far, compact[0], compact[1]]
+    halves = np.concatenate(blocks, axis=0)
+    places = np.concatenate([block.T for block in blocks], axis=1)
+    small = np.zeros((192, 256), np.float32)
+    small[0:128, :128] = pool
+    small[0:128, 128:256] = pool.T
+    for x in range(3):
         for r in range(4):
-            fold[8 * i + r, 4 * i + r] = 1.0
+            small[128 + 4 * x + r, 64 * x + 16 * r : 64 * x + 16 * r + 16] = 1.0
         for r in range(2):
-            for j in range(2):
-                fold[8 * i + 4 + r, 64 + 32 * j + 2 * i + r] = 1.0
-        for j in range(4):
-            fold[8 * i + 6, 128 + 16 * j + i] = 1.0
-    halves = np.concatenate([wide, pick[0], pick[1], compact[0], compact[1], fold], axis=0)
+            small[144 + 4 * x + r, 64 * x + 32 * r : 64 * x + 32 * r + 32] = 1.0
+        small[146 + 4 * x : 148 + 4 * x, 64 * x : 64 * x + 64] = 1.0
+    for r in range(32):
+        small[160 + r, r] = 1.0
+        small[160 + r, 32 + r // 2] = 2.0**-0.5
     ancestor = np.where(pool.T > 0, 0.0, LOW)
     row_scale = np.where(level_of < 8, 2.0 ** (-level_of / 2.0), 0.0)[:, None] * np.ones((1, 128))
+    half_scale = 2.0 ** (-np.array([4] * 16 + [5, 5, 6, 7] * 4) / 2.0)
     shard = np.arange(128) // 8
     across = np.where(shard[:, None] // 8 != shard[None, :] // 8, 0.0, LOW)
     near = np.full((48, 256), LOW)
@@ -73,23 +85,24 @@
         [
             np.concatenate([ancestor, row_scale], axis=1),
             np.concatenate([np.eye(128), across], axis=1),
+            np.repeat(half_scale[:, None], 256, axis=1),
             near,
             far,
         ],
         axis=0,
     )
-    return halves.astype(np.float32), singles.astype(np.float32)
-
-
-T_POOL, T_PICK, T_COMPACT, T_FOLD = 0, 128, 384, 640
-T_ROWS = 768
-S_ANC, S_DIAG, S_NEAR, S_FAR = 0, 128, 256, 304
-S_ROWS = 432
+    return small, halves, places, singles.astype(np.float32)
+
+
+T_POOL, T_HALF, T_GATHER = 0, 128, 160
+P_PICK, P_FAR, P_COMPACT = 0, 384, 512
+S_ANC, S_DIAG, S_HALF, S_NEAR, S_FAR = 0, 128, 256, 288, 336
+S_ROWS = 464
 
 C_ENTRY, C_EXIT, C_ONE, C_SHARE, C_PART, C_ONE_BACK = 0, 4, 8, 9, 10, 11
 C_NEAR, C_NEAR_BACK, C_FAR, C_FAR_BACK = 11, 14, 17, 24
-C_ROWS, C_QUERY, C_SUMS, C_ADJ, C_DQUERY, C_DROWS = 32, 48, 64, 80, 96, 112
-COPIES = 128
+C_ROWS, C_SUMS, C_ADJ, C_DROWS, C_COARSE = 32, 64, 80, 96, 128
+COPIES = 129
 
 
 def mm(a, b):
@@ -115,15 +128,15 @@
 def kernel(
     heads,
     unroll,
-    key_hbm, value_hbm, query_hbm, grad_hbm, half_hbm, single_hbm,
-    att_hbm, dquery_hbm, dkey_hbm, dvalue_hbm,
-    half_tab, single_tab, rows_in, coarse_kv, coarse_q, one_kv, near_kv,
-    rows_send, rows_recv, query_send, query_recv, far_send, far_kv, pair_kv,
+    key_hbm, value_hbm, query_hbm, grad_hbm, small_hbm, half_hbm, place_hbm, single_hbm,
+    att_hbm, dquery_hbm, dkey_hbm, dvalue_hbm, coarse_hbm, far_hbm,
+    small_tab, half_tab, place_tab, single_tab, raw_in, rows_in, coarse_kv, coarse_q, one_kv, near_kv,
+    rows_send, rows_recv, far_q, far_send, far_kv, pair_kv,
     local_scores, local_dprob, expo_one, expo_near, expo_far, numer, tops, totals,
-    sums_send, sums_recv, adj_send, adj_recv, dquery_send, dquery_recv, drows_send, drows_recv,
+    sums_send, sums_recv, adj_send, adj_recv, dfar_q, drows_send,
     dfar_send, dfar_recv,
-    att_buf, dquery_buf, dkv_buf, local_ds, local_probs, adjoint, offset, dcoarse_q, dlocal_kv,
-    part_grad, swap_grad, send_grad, recv_grad, one_part, one_recv,
+    att_buf, dquery_buf, dkv_buf, local_ds, local_probs, adjoint, offset, dcoarse_q,
+    part_grad, swap_grad, send_grad, recv_grad, one_part, one_recv, coarse_grad,
     load_sem, store_sem, self_sem, send_sem, recv_sem,
 ):
     seq = lax.axis_index("seq")
@@ -159,9 +172,17 @@
         for i, ref in enumerate(sources)
     ]
     table_loads = [
-        pltpu.make_async_copy(half_hbm, half_tab, load_sem.at[4]),
+        pltpu.make_async_copy(small_hbm, small_tab, load_sem.at[4]),
         pltpu.make_async_copy(single_hbm, single_tab, load_sem.at[5]),
-    ]
+        pltpu.make_async_copy(half_hbm, half_tab, load_sem.at[9]),
+        pltpu.make_async_copy(place_hbm, place_tab, load_sem.at[10]),
+    ]
+    raw_loads = [
+        pltpu.make_async_copy(ref, raw_in.at[pl.ds(64 * i, 64)], load_sem.at[6 + i]) for i, ref in enumerate(sources[:3])
+    ]
+    coarse_store = pltpu.make_async_copy(coarse_grad.at[0], coarse_hbm.at[:, mine], store_sem.at[4])
+    coarse_exit = remote(coarse_grad.at[1], coarse_hbm.at[:, mine], C_COARSE, mate)
+    coarse_wait = remote(coarse_grad.at[1], coarse_hbm.at[:, theirs], C_COARSE, mate)
     entry = [
         remote(ref.at[:, theirs], rows_in.at[i, pl.ds(64, 64)], C_ENTRY + i, mate)
         for i, ref in enumerate(sources)
@@ -225,12 +246,46 @@
                 self.out.append(remote(send.at[slab(slot, rows)], recv.at[chip, core], base + m, device))
                 self.come.append(remote(send.at[slab(slot, rows)], recv.at[owner, group], base + m, device))
 
-    rows_out = Spread(0, C_ROWS, rows_send, rows_recv, 16)
-    query_out = Spread(1, C_QUERY, query_send, query_recv, 8)
-    sums_back = Return(2, C_SUMS, sums_send, sums_recv, 16)
-    adj_out = Spread(3, C_ADJ, adj_send, adj_recv, 16)
-    dquery_back = Return(4, C_DQUERY, dquery_send, dquery_recv, 8)
-    drows_back = Return(5, C_DROWS, drows_send, drows_recv, 16)
+    class Rows:
+        def __init__(self, which, base, pairs):
+            self.local = pltpu.make_async_copy(*pairs(0, 0)[:2], self_sem.at[which])
+            self.out = []
+            self.come = []
+            for side in (0, 1):
+                for m in range(PLANE):
+                    if side == 0 and m == 0:
+                        continue
+                    src, dst, land = pairs(side, m)
+                    device = (peers[m][0][0], mate[1] if side else head)
+                    self.out.append(remote(src, dst, base + 16 * side + m, device))
+                    self.come.append(remote(src, land, base + 16 * side + m, device))
+
+        start = Spread.start
+        wait_recv = Spread.wait_recv
+        wait_send = Spread.wait_send
+
+    def message_pairs(side, m):
+        _, slot, owner, group = peers[m]
+        group_of_heads = mate[1] if side else head
+        return (
+            rows_send.at[group_of_heads * heads + owner, group],
+            rows_recv.at[slab(2 * place + side, 16)],
+            rows_recv.at[slab(2 * slot + side, 16)],
+        )
+
+    def drow_pairs(side, m):
+        _, slot, owner, group = peers[m]
+        group_of_heads = mate[1] if side else head
+        return (
+            drows_send.at[slab(2 * slot + side, 16)],
+            far_hbm.at[slab(2 * (head * heads + chip) + core, 16)],
+            far_hbm.at[slab(2 * (group_of_heads * heads + owner) + group, 16)],
+        )
+
+    rows_out = Rows(0, C_ROWS, message_pairs)
+    sums_back = Return(1, C_SUMS, sums_send, sums_recv, 16)
+    adj_out = Spread(2, C_ADJ, adj_send, adj_recv, 16)
+    drows_back = Rows(3, C_DROWS, drow_pairs)
 
     results = ((att_buf, att_hbm), (dquery_buf, dquery_hbm), (dkv_buf.at[0], dkey_hbm), (dkv_buf.at[1], dvalue_hbm))
     stores = [
@@ -246,36 +301,68 @@
         for i, (buf, out) in enumerate(results)
     ]
 
-    for copy in loads + table_loads:
+    for copy in raw_loads + table_loads + loads:
         copy.start()
     barrier = pltpu.get_barrier_semaphore()
-    partners = [mate] + [peer[0] for peer in peers[1:]] + list(far_dev.values())
+    partners = [peer[0] for peer in peers[1:]] + [(peer[0][0], mate[1]) for peer in peers] + list(far_dev.values())
     for device in partners:
         pl.semaphore_signal(barrier, inc=1, device_id=device, device_id_type=MESH)
-    pl.semaphore_wait(barrier, len(partners))
-    for copy in entry:
-        copy.start()
-
     def columns(h):
         return pl.ds(pl.multiple_of(h * DH, DH), DH)
 
-    def each_head(*steps):
+    def each_head(*steps, count=heads):
         def body(i, carry):
             for step in steps:
                 for j in range(unroll):
                     step(i * unroll + j)
             return carry
 
-        lax.fori_loop(0, heads // unroll, body, 0)
-
-    for copy in table_loads:
+        lax.fori_loop(0, count // unroll, body, 0)
+
+    for copy in table_loads[:2]:
         copy.wait()
     everything = pl.ds(0, 128)
     right = pl.ds(128, 128)
 
+    for copy in raw_loads:
+        copy.wait()
+
+    def pool_half(h):
+        rows = mm(small_tab[pl.ds(T_HALF, 32), pl.ds(0, 192)], raw_in[:, columns(h)])
+        rows = (rows * single_tab[pl.ds(S_HALF, 32), everything]).astype(BF16)
+        rows_send[h, 0] = rows[0:16]
+        rows_send[h, 1] = rows[16:32]
+
+    each_head(pool_half, count=2 * heads)
+    pl.semaphore_wait(barrier, len(partners))
+    rows_out.start()
+    for copy in entry:
+        copy.start()
+
     def pooled(which, h):
-        rows = mm(half_tab[pl.ds(T_POOL, 128), pl.ds(0, 128)], rows_in[which, :, columns(h)])
-        return rows * single_tab[pl.ds(S_ANC, 128), right]
+        rows = mm(small_tab[pl.ds(T_POOL, 112), pl.ds(0, 128)], rows_in[which, :, columns(h)])
+        return (rows * single_tab[pl.ds(S_ANC, 112), right]).astype(BF16)
+
+    for copy in table_loads[2:]:
+        copy.wait()
+    rows_out.wait_recv()
+
+    def picked(row, count):
+        return mm(half_tab[pl.ds(row, count)], rows_recv[...]).astype(BF16)
+
+    @pl.when(core == 1)
+    def _():
+        for kv in (0, 1):
+            far_send[:, pl.ds(128 * kv, 128)] = picked(P_COMPACT + 128 * kv, 112)
+        for copy in far_copies:
+            copy.start()
+        far_q[...] = picked(P_FAR, 128)
+
+    @pl.when(core == 0)
+    def _():
+        for kv in (0, 1):
+            pair_kv[:, pl.ds(128 * kv, 128)] = picked(P_PICK + 128 * kv, 128)
+        far_q[...] = picked(P_PICK + 256, 128)
 
     for kv in (0, 1):
         loads[kv].wait()
@@ -283,17 +370,10 @@
 
     def pool_rows(h):
         cols = columns(h)
-        keys = pooled(0, h)
-        vals = pooled(1, h)
-        coarse_kv[0, :, cols] = keys.astype(BF16)
-        coarse_kv[1, :, cols] = vals.astype(BF16)
-        for group in (0, 1):
-            low = 112 + 8 * group
-            both = jnp.concatenate([keys[low : low + 8], vals[low : low + 8]], axis=0)
-            rows_send[h, group] = both.astype(BF16)
+        coarse_kv[0, :, cols] = pooled(0, h)
+        coarse_kv[1, :, cols] = pooled(1, h)
 
     each_head(pool_rows)
-    rows_out.start()
     for copy in near_copies:
         copy.start()
     one_swap.start()
@@ -302,30 +382,9 @@
     entry[2].wait_recv()
 
     def pool_queries(h):
-        rows = pooled(2, h)
-        short = rows.astype(BF16)
-        coarse_q[:, columns(h)] = short
-        for group in (0, 1):
-            query_send[h, group] = short.astype(F32)[112 + 8 * group : 120 + 8 * group]
+        coarse_q[:, columns(h)] = pooled(2, h)
 
     each_head(pool_queries)
-    query_out.start()
-
-    rows_out.wait_recv()
-
-    @pl.when(core == 1)
-    def _():
-        for kv in (0, 1):
-            rows = mm(half_tab[pl.ds(T_COMPACT + 128 * kv, 112)], rows_recv[...])
-            far_send[:, pl.ds(128 * kv, 128)] = rows.astype(BF16)
-        for copy in far_copies:
-            copy.start()
-
-    @pl.when(core == 0)
-    def _():
-        for kv in (0, 1):
-            rows = mm(half_tab[pl.ds(T_PICK + 128 * kv, 128)], rows_recv[...])
-            pair_kv[:, pl.ds(128 * kv, 128)] = rows.astype(BF16)
 
     def to_row(column, start):
         count = column.shape[0]
@@ -370,16 +429,8 @@
         tops[h, pl.ds(1, 1)] = to_row(top, 64)
         totals[h, pl.ds(1, 1)] = to_row(total, 64)
 
-    one_swap.wait_recv()
-    each_head(forward_one)
-    for copy in near_copies:
-        copy.wait_recv()
-    share.start()
-
-    query_out.wait_recv()
-
     def forward_far(keys, vals, mask, span):
-        weights, top, total, sums = attend(query_recv[...].astype(BF16), keys, vals, mask)
+        weights, top, total, sums = attend(far_q[...], keys, vals, mask)
         expo_far[:, pl.ds(0, span)] = weights
         lanes = lax.broadcasted_iota(jnp.int32, (128, 128), 1)
         pair = jnp.where(lanes < 64, top, total)
@@ -401,6 +452,12 @@
         )
 
     sums_back.start()
+
+    one_swap.wait_recv()
+    each_head(forward_one)
+    for copy in near_copies:
+        copy.wait_recv()
+    share.start()
 
     loads[3].wait()
     entry[3].wait_recv()
@@ -480,120 +537,108 @@
 
     each_head(backward_near)
     part_swap.start()
+    each_head(backward_one)
+    one_back.start()
+
+    def unpooled(rows):
+        count = rows.shape[0]
+        scaled = rows * single_tab[pl.ds(S_ANC, count), right]
+        return mm(small_tab[pl.ds(T_POOL, 128), pl.ds(128, count)], scaled.astype(BF16))
+
+    def query_total(h):
+        cols = columns(h)
+        total = mm(local_ds[h], rows_in[0, :, cols]) + unpooled(dcoarse_q[h])
+        dquery_buf[:, cols] = (total * SCALE).astype(BF16)
+
+    each_head(query_total)
+    stores[1].start()
+    exits[1].start()
+    part_swap.wait_recv()
+
+    def sum_near(h):
+        cols = columns(h)
+        for kv in (0, 1):
+            both = part_grad[0, kv, :, cols].astype(F32) + swap_grad[kv, :, cols].astype(F32)
+            send_grad[kv, :, cols] = both.astype(BF16)
+
+    each_head(sum_near)
+    for copy in near_back:
+        copy.start()
+    one_back.wait_recv()
+
+    def local_back(h):
+        cols = columns(h)
+        dkeys = mm_tn(local_ds[h], rows_in[2, :, cols]) * SCALE
+        dvals = mm_tn(local_probs[h], rows_in[3, :, cols])
+        for kv, total in ((0, dkeys), (1, dvals)):
+            total = total + unpooled(one_recv[kv, :, cols].astype(F32))
+            dkv_buf[kv, :, cols] = total.astype(BF16)
+
+    each_head(local_back)
+    for i in (2, 3):
+        stores[i].start()
+        exits[i].start()
+
     adj_out.wait_recv()
 
     def backward_far(keys, vals, span):
         arrived = adj_recv[...].reshape(PLANE, 16, 128)
         adj = arrived[:, 0:8].reshape(128, 128).astype(BF16)
         shift = arrived[:, 8:16].reshape(128, 128)[:, 0:1]
-        return attend_back(
-            expo_far[:, pl.ds(0, span)], adj, shift, query_recv[...].astype(BF16), keys, vals
-        )
-
-    def put_rows(dkeys, dvals):
-        whole = jnp.concatenate([dkeys.reshape(PLANE, 8, 128), dvals.reshape(PLANE, 8, 128)], axis=1)
-        drows_send[...] = whole.reshape(PLANE * 16, 128)
+        dqueries, dkeys, dvals = attend_back(expo_far[:, pl.ds(0, span)], adj, shift, far_q[...], keys, vals)
+        return (dqueries * SCALE).astype(BF16), dkeys.astype(BF16), dvals.astype(BF16)
 
     @pl.when(core == 0)
     def _():
         dqueries, dkeys, dvals = backward_far(pair_kv[:, everything], pair_kv[:, right], 128)
-        dquery_send[...] = dqueries
-        put_rows(dkeys, dvals)
+        rows = jnp.concatenate([dkeys, dvals, dqueries], axis=0)
+        drows_send[...] = mm(place_tab[:, pl.ds(P_PICK, 384)], rows).astype(BF16)
 
     @pl.when(core == 1)
     def _():
         dqueries, dkeys, dvals = backward_far(far_kv[:, everything], far_kv[:, right], 192)
-        dquery_send[...] = dqueries
-        dfar_send[:, everything] = dkeys.astype(BF16)
-        dfar_send[:, right] = dvals.astype(BF16)
+        dfar_send[:, everything] = dkeys
+        dfar_send[:, right] = dvals
         for copy in far_back:
             copy.start()
-
-    dquery_back.start()
-
-    @pl.when(core == 0)
-    def _():
-        for copy in drows_back.out:
-            copy.start()
-        drows_back.local.start()
-
-    part_swap.wait_recv()
-
-    def sum_near(h):
-        cols = columns(h)
-        for kv in (0, 1):
-            both = part_grad[0, kv, :, cols].astype(F32) + swap_grad[kv, :, cols].astype(F32)
-            send_grad[kv, :, cols] = both.astype(BF16)
-
-    each_head(sum_near)
-    for copy in near_back:
-        copy.start()
-    each_head(backward_one)
-    one_back.start()
-
-    @pl.when(core == 1)
-    def _():
+        dfar_q[...] = dqueries
         for copy in far_back:
             copy.wait_recv()
-        both = mm(half_tab[pl.ds(T_FOLD, 128), pl.ds(0, 192)], dfar_recv[...])
-        put_rows(both[:, 0:128], both[:, 128:256])
-        for copy in drows_back.out:
-            copy.start()
-        drows_back.local.start()
-
-    dquery_back.wait_recv()
-
-    def unpooled(rows):
-        scaled = rows * single_tab[pl.ds(S_ANC, 128), right]
-        return mm(half_tab[pl.ds(T_POOL, 128), right], scaled.astype(BF16))
-
-    def query_total(h):
-        cols = columns(h)
-        coarse = jnp.concatenate([dcoarse_q[h], dquery_recv[h, 0], dquery_recv[h, 1]], axis=0)
-        total = mm(local_ds[h], rows_in[0, :, cols]) + unpooled(coarse)
-        dquery_buf[:, cols] = (total * SCALE).astype(BF16)
-
-    each_head(query_total)
-    stores[1].start()
-    exits[1].start()
-
-    def local_back(h):
-        cols = columns(h)
-        dlocal_kv[0, :, cols] = mm_tn(local_ds[h], rows_in[2, :, cols]) * SCALE
-        dlocal_kv[1, :, cols] = mm_tn(local_probs[h], rows_in[3, :, cols])
-
-    each_head(local_back)
-    one_back.wait_recv()
+        came = dfar_recv[...].astype(F32)
+        level_six = came[64:96] + came[96:128]
+        level_seven = (came[128:144] + came[144:160]) + (came[160:176] + came[176:192])
+        rows = jnp.concatenate([came[0:64], level_six, level_seven, jnp.zeros((16, 256), F32)], axis=0).astype(BF16)
+        rows = jnp.concatenate([dfar_q[...], rows[:, 0:128], rows[:, 128:256]], axis=0)
+        drows_send[...] = mm(place_tab[:, pl.ds(P_FAR, 384)], rows).astype(BF16)
+
+    drows_back.start()
+
     for copy in near_back:
         copy.wait_recv()
-    drows_back.wait_recv()
-
-    def finish(kv):
-        def step(h):
-            cols = columns(h)
+
+    def gather_coarse(h):
+        cols = columns(h)
+        for kv in (0, 1):
             coarse = jnp.concatenate(
                 [
-                    one_recv[kv, :, cols].astype(F32),
                     recv_grad[kv, pl.ds(0, 32), cols].astype(F32),
                     recv_grad[kv, pl.ds(32, 16), cols].astype(F32)
                     + recv_grad[kv, pl.ds(48, 16), cols].astype(F32),
-                    drows_recv[h, 0, pl.ds(8 * kv, 8)],
-                    drows_recv[h, 1, pl.ds(8 * kv, 8)],
                 ],
                 axis=0,
             )
-            dkv_buf[kv, :, cols] = (dlocal_kv[kv, :, cols] + unpooled(coarse)).astype(BF16)
-
-        return step
-
-    for kv in (0, 1):
-        each_head(finish(kv))
-        stores[2 + kv].start()
-        exits[2 + kv].start()
-
-    for copy in entry + near_copies + near_back + [one_swap, share, part_swap, one_back] + exits:
+            total = mm(small_tab[pl.ds(T_GATHER, 32), pl.ds(0, 48)], coarse.astype(BF16)).astype(BF16)
+            coarse_grad[0, pl.ds(16 * kv, 16), cols] = total[0:16]
+            coarse_grad[1, pl.ds(16 * kv, 16), cols] = total[16:32]
+
+    each_head(gather_coarse)
+    coarse_store.start()
+    coarse_exit.start()
+    drows_back.wait_recv()
+
+    for copy in entry + near_copies + near_back + [one_swap, share, part_swap, one_back, coarse_exit] + exits:
         copy.wait_send()
-    for copy in (rows_out, query_out, sums_back, adj_out, dquery_back, drows_back):
+    for copy in (rows_out, sums_back, adj_out, drows_back):
         copy.wait_send()
 
     @pl.when(core == 1)
@@ -601,15 +646,44 @@
         for copy in far_copies + far_back:
             copy.wait_send()
 
-    for copy in stores:
+    for copy in stores + [coarse_store]:
         copy.wait()
-    for copy in exit_waits:
+    for copy in exit_waits + [coarse_wait]:
         copy.wait_recv()
 
 
+def last_kernel(
+    heads, att_ref, dquery_ref, dkey_ref, dvalue_ref, coarse_ref, far_ref, att_out, dquery_out, dkey_out, dvalue_out
+):
+    att_out[...] = att_ref[...]
+    rows = lax.broadcasted_iota(jnp.int32, (64, 32), 0)
+    parents = lax.broadcasted_iota(jnp.int32, (64, 32), 1)
+
+    def among(first, count, span):
+        at = parents - first
+        return (at >= 0) & (at < count) & (rows >= span * at) & (rows < span * at + span)
+
+    spread = jnp.where(among(0, 16, 4), 0.5, 0.0).astype(BF16)[:, 0:16]
+    far = [
+        jnp.where(among(4 * x, 4, 16), 0.25, 0.0)
+        + jnp.where(among(16 + 4 * x, 2, 32), 2.0**-2.5, 0.0)
+        + jnp.where(among(18 + 4 * x, 1, 64), 2.0**-3, 0.0)
+        + jnp.where(among(19 + 4 * x, 1, 64), 2.0**-3.5, 0.0)
+        for x in range(3)
+    ]
+    far = jnp.concatenate(far, axis=0).astype(BF16)
+    for h in range(heads):
+        cols = pl.ds(DH * h, DH)
+        added = mm(far, far_ref[pl.ds(32 * h, 32)])
+        near = [mm(spread, coarse_ref[pl.ds(16 * kv, 16), cols]) for kv in (0, 1)]
+        dkey_out[:, cols] = (dkey_ref[:, cols].astype(F32) + added[0:64] + near[0]).astype(BF16)
+        dvalue_out[:, cols] = (dvalue_ref[:, cols].astype(F32) + added[64:128] + near[1]).astype(BF16)
+        dquery_out[:, cols] = (dquery_ref[:, cols].astype(F32) + added[128:192]).astype(BF16)
+
+
 def solution(mesh):
-    halves, singles = tables()
-    halves = halves.astype(BF16)
+    small, halves, places, singles = tables()
+    small, halves, places = (table.astype(BF16) for table in (small, halves, places))
     unroll = 4
 
     def local(queries, key_rows, values, out_grad):
@@ -621,17 +695,19 @@
         out = jax.ShapeDtypeStruct((rows, columns), BF16)
         vmem = pltpu.VMEM
         scratch = [
-            vmem((T_ROWS, 256), BF16),
+            vmem((192, 256), BF16),
+            vmem((768, 512), BF16),
+            vmem((512, 768), BF16),
             vmem((S_ROWS, 256), F32),
+            vmem((3 * rows, columns), BF16),
             vmem((4, tall, width), BF16),
-            vmem((2, 128, width), BF16),
-            vmem((128, width), BF16),
+            vmem((2, 112, width), BF16),
+            vmem((112, width), BF16),
             vmem((2, 64, width), BF16),
             vmem((2, 2, 64, width), BF16),
-            vmem((heads, 2, 16, 128), BF16),
-            vmem((PLANE * 16, 128), BF16),
-            vmem((heads, 2, 8, 128), F32),
-            vmem((PLANE * 8, 128), F32),
+            vmem((2 * heads, 2, 16, 128), BF16),
+            vmem((PLANE * 32, 128), BF16),
+            vmem((128, 128), BF16),
             vmem((112, 256), BF16),
             vmem((192, 256), BF16),
             vmem((128, 256), BF16),
@@ -647,10 +723,8 @@
             vmem((heads, 2, 16, 128), F32),
             vmem((heads, 2, 16, 128), F32),
             vmem((PLANE * 16, 128), F32),
-            vmem((PLANE * 8, 128), F32),
-            vmem((heads, 2, 8, 128), F32),
-            vmem((PLANE * 16, 128), F32),
-            vmem((heads, 2, 16, 128), F32),
+            vmem((128, 128), BF16),
+            vmem((PLANE * 32, 128), BF16),
             vmem((192, 256), BF16),
             vmem((192, 256), BF16),
             vmem((tall, width), BF16),
@@ -661,30 +735,39 @@
             vmem((heads, 128, 128), BF16),
             vmem((heads, 128, 128), F32),
             vmem((heads, 112, 128), F32),
-            vmem((2, tall, width), F32),
             vmem((2, 2, 64, width), BF16),
             vmem((2, 64, width), BF16),
             vmem((2, 64, width), BF16),
             vmem((2, 64, width), BF16),
             vmem((2, 64, width), BF16),
             vmem((2, 64, width), BF16),
-            pltpu.SemaphoreType.DMA((6,)),
+            vmem((2, 32, width), BF16),
+            pltpu.SemaphoreType.DMA((11,)),
+            pltpu.SemaphoreType.DMA((5,)),
             pltpu.SemaphoreType.DMA((4,)),
-            pltpu.SemaphoreType.DMA((6,)),
             pltpu.SemaphoreType.DMA((COPIES,)),
             pltpu.SemaphoreType.DMA((COPIES,)),
         ]
-        return pl.pallas_call(
+        parts = pl.pallas_call(
             functools.partial(kernel, heads, unroll),
-            out_shape=(out,) * 4,
-            in_specs=[anywhere] * 6,
-            out_specs=(anywhere,) * 4,
+            out_shape=(out,) * 4
+            + (jax.ShapeDtypeStruct((32, columns), BF16), jax.ShapeDtypeStruct((64 * heads, 128), BF16)),
+            in_specs=[anywhere] * 8,
+            out_specs=(anywhere,) * 6,
             scratch_shapes=scratch,
             compiler_params=pltpu.CompilerParams(
                 collective_id=0, has_side_effects=True, vmem_limit_bytes=60 << 20
             ),
             name="sibling_attention",
-        )(key_rows, values, queries, out_grad, jnp.asarray(halves), jnp.asarray(singles))
+        )(key_rows, values, queries, out_grad, *(jnp.asarray(table) for table in (small, halves, places, singles)))
+        whole = pl.BlockSpec(memory_space=pltpu.VMEM)
+        return pl.pallas_call(
+            functools.partial(last_kernel, 2 * heads),
+            out_shape=(out,) * 4,
+            in_specs=[whole] * 6,
+            out_specs=(whole,) * 4,
+            name="coarse_rows_added",
+        )(*parts)
 
     spec = P(("seq", "head"), None)
     return jax.shard_map(

time: 66.8 us -> 56 us (0.84)
  Pallas kernels: 61.5 us -> 55.2 us
  local copies, waits for them, and re-layouts: 4.5 us -> 0 us
    pallas_call x1, Pallas kernels: 61.5 us -> 52.5 us  [local(): pl.pallas_call(functools.partial(kernel, heads, unroll), out_shape=(out,)...]
    unnamed x10 -> x0, local copies, waits for them, and re-layouts: 4.5 us -> none
    pallas_call x0 -> x1, Pallas kernels: none -> 2.71 us  [local(): pl.pallas_call(functools.partial(last_kernel, 2 * heads), out_shape=(out,...]
where the time goes in v3:
time: 56 us; the launch traced here: 55.9 us
  Pallas kernels  55.2 us (99%)
  between operations  0.64 us (1%)
    pallas_call x1, Pallas kernels, local(): pl.pallas_call(functools.partial(kernel, heads, unroll), out_shape=(out,)...  52.5 us
    pallas_call x1, Pallas kernels, local(): pl.pallas_call(functools.partial(last_kernel, 2 * heads), out_shape=(out,...  2.71 us

profile of v3, /device:TPU:1, one launch (start us, length us, event | category | flops | bytes accessed | tf_op | source)
XLA Modules:
  0.0 55.9 jit_solution(10650080472570184778)
XLA Ops:
  0.6 52.5 %sibling_attention.1 = (bf16[64,2048]{1,0:T(8,128)(2,1)}, bf16[64,2048]{1,0:T(8,128)(2,1)}, bf16[64,2048]{1,0:T(8,128)(2,1)}, bf16[64,2048]{1,0:T(8,128)(2,1)}, ...) custom-call(bf16[64,2048]{1,0:T(8,128)(2,1)} %key_hbm.1, bf16[64,2048]{1,0:T(8,128)(2,1)} %value_hbm.1, ...), custom_call_target="tpu_custom_call" | custom-call | tf_op jit(solution)/shard_map/sibling_attention/pallas_call | solution.py:751
  53.2 2.7 %coarse_rows_added.1 = (bf16[64,2048]{1,0:T(8,128)(2,1)}, bf16[64,2048]{1,0:T(8,128)(2,1)}, bf16[64,2048]{1,0:T(8,128)(2,1)}, bf16[64,2048]{1,0:T(8,128)(2,1)}) custom-call(bf16[64,2048]{1,0:T(8,128)(2,1)} %get-tuple-element.10.att_ref, bf16[64,2048]{1,0:T(8,128)(2,1)} %get-tuple-element.11.dquery_ref, bf16[64,2048]{1,0:T(8,128)(2,1)} %get-tuple-element.12.dkey_ref, ...), custom_call_target="tpu_custom_call" | custom-call | tf_op jit(solution)/shard_map/coarse_rows_added/pallas_call | solution.py:764

commit v4 on v3

--- a/solution.py
+++ b/solution.py
@@ -127,7 +127,6 @@
 
 def kernel(
     heads,
-    unroll,
     key_hbm, value_hbm, query_hbm, grad_hbm, small_hbm, half_hbm, place_hbm, single_hbm,
     att_hbm, dquery_hbm, dkey_hbm, dvalue_hbm, coarse_hbm, far_hbm,
     small_tab, half_tab, place_tab, single_tab, raw_in, rows_in, coarse_kv, coarse_q, one_kv, near_kv,
@@ -308,16 +307,12 @@
     for device in partners:
         pl.semaphore_signal(barrier, inc=1, device_id=device, device_id_type=MESH)
     def columns(h):
-        return pl.ds(pl.multiple_of(h * DH, DH), DH)
+        return pl.ds(h * DH, DH)
 
     def each_head(*steps, count=heads):
-        def body(i, carry):
-            for step in steps:
-                for j in range(unroll):
-                    step(i * unroll + j)
-            return carry
-
-        lax.fori_loop(0, count // unroll, body, 0)
+        for step in steps:
+            for h in range(count):
+                step(h)
 
     for copy in table_loads[:2]:
         copy.wait()
@@ -409,25 +404,29 @@
     def near_rows(kv, h):
         return jnp.concatenate([near_kv[0, kv, :, columns(h)], near_kv[1, kv, :, columns(h)]], axis=0)
 
-    def forward_one(h):
-        cols = columns(h)
-        weights, top, total, sums = attend(
-            coarse_q[pl.ds(0, 64), cols], one_kv[0, :, cols], one_kv[1, :, cols], None
-        )
-        expo_one[h] = weights
-        numer[h, pl.ds(0, 64)] = sums
-        tops[h, pl.ds(0, 1)] = to_row(top, 0)
-        totals[h, pl.ds(0, 1)] = to_row(total, 0)
-
-    def forward_near(h):
-        weights, top, total, sums = attend(
-            coarse_q[pl.ds(64, 48), columns(h)], near_rows(0, h), near_rows(1, h),
-            single_tab[pl.ds(S_NEAR, 48), everything],
-        )
-        expo_near[h] = weights
-        numer[h, pl.ds(64, 48)] = sums
-        tops[h, pl.ds(1, 1)] = to_row(top, 64)
-        totals[h, pl.ds(1, 1)] = to_row(total, 64)
+    def forward_all(group, start, rows, keys_of, mask, expo):
+        every = range(heads)
+        scores = [mm_nt(coarse_q[pl.ds(start, rows), columns(h)], keys_of(0, h)) * SCALE for h in every]
+        if mask is not None:
+            scores = [score + mask for score in scores]
+        top = [jnp.max(score, axis=1, keepdims=True) for score in scores]
+        weights = [jnp.exp(scores[h] - top[h]) for h in every]
+        total = [jnp.sum(weight, axis=1, keepdims=True) for weight in weights]
+        for h in every:
+            expo[h] = weights[h]
+            numer[h, pl.ds(start, rows)] = mm(weights[h].astype(BF16), keys_of(1, h))
+        for h in every:
+            tops[h, pl.ds(group, 1)] = to_row(top[h], start)
+            totals[h, pl.ds(group, 1)] = to_row(total[h], start)
+
+    def one_rows(kv, h):
+        return one_kv[kv, :, columns(h)]
+
+    def forward_one():
+        forward_all(0, 0, 64, one_rows, None, expo_one)
+
+    def forward_near():
+        forward_all(1, 64, 48, near_rows, single_tab[pl.ds(S_NEAR, 48), everything], expo_near)
 
     def forward_far(keys, vals, mask, span):
         weights, top, total, sums = attend(far_q[...], keys, vals, mask)
@@ -454,7 +453,7 @@
     sums_back.start()
 
     one_swap.wait_recv()
-    each_head(forward_one)
+    forward_one()
     for copy in near_copies:
         copy.wait_recv()
     share.start()
@@ -469,7 +468,7 @@
 
     each_head(score_local)
     share.wait_recv()
-    each_head(forward_near)
+    forward_near()
     sums_back.wait_recv()
 
     def combine(h):
@@ -497,12 +496,14 @@
         weight = (factor * inverse).astype(BF16)
         local_probs[h] = probs.astype(BF16)
         local_ds[h] = (probs * (local_dprob[h] - dots)).astype(BF16)
-        adj = mm_tn(weight, grad)
+        lane = lax.broadcasted_iota(jnp.int32, (128, 128), 1)
+        dots_wide = jnp.broadcast_to(dots, (128, 128))
+        dots_high = dots_wide.astype(BF16).astype(F32)
+        dots_pair = jnp.where(lane < 64, dots_high, dots_wide - dots_high).astype(BF16)
+        both = mm_tn(weight, jnp.concatenate([grad, dots_pair], axis=1))
+        adj = both[:, 0:128]
+        shift = both[:, 128:256]
         adjoint[h] = adj.astype(BF16)
-        dots_wide = jnp.broadcast_to(dots, (128, 128))
-        dots_high = dots_wide.astype(BF16)
-        dots_low = (dots_wide - dots_high.astype(F32)).astype(BF16)
-        shift = mm_tn(weight, dots_high) + mm_tn(weight, dots_low)
         offset[h] = shift
         for group in (0, 1):
             low = 112 + 8 * group
@@ -514,10 +515,13 @@
     stores[0].start()
     exits[0].start()
 
+    def shift_of(h, start, count):
+        return offset[h, pl.ds(start, count), pl.ds(0, 1)] + offset[h, pl.ds(start, count), pl.ds(64, 1)]
+
     def backward_near(h):
         cols = columns(h)
         dqueries, dkeys, dvals = attend_back(
-            expo_near[h], adjoint[h, pl.ds(64, 48)], offset[h, pl.ds(64, 48), pl.ds(0, 1)],
+            expo_near[h], adjoint[h, pl.ds(64, 48)], shift_of(h, 64, 48),
             coarse_q[pl.ds(64, 48), cols], near_rows(0, h), near_rows(1, h),
         )
         dcoarse_q[h, pl.ds(64, 48)] = dqueries
@@ -528,7 +532,7 @@
     def backward_one(h):
         cols = columns(h)
         dqueries, dkeys, dvals = attend_back(
-            expo_one[h], adjoint[h, pl.ds(0, 64)], offset[h, pl.ds(0, 64), pl.ds(0, 1)],
+            expo_one[h], adjoint[h, pl.ds(0, 64)], shift_of(h, 0, 64),
             coarse_q[pl.ds(0, 64), cols], one_kv[0, :, cols], one_kv[1, :, cols],
         )
         dcoarse_q[h, pl.ds(0, 64)] = dqueries
@@ -584,7 +588,8 @@
     def backward_far(keys, vals, span):
         arrived = adj_recv[...].reshape(PLANE, 16, 128)
         adj = arrived[:, 0:8].reshape(128, 128).astype(BF16)
-        shift = arrived[:, 8:16].reshape(128, 128)[:, 0:1]
+        shift = arrived[:, 8:16].reshape(128, 128)
+        shift = shift[:, 0:1] + shift[:, 64:65]
         dqueries, dkeys, dvals = attend_back(expo_far[:, pl.ds(0, span)], adj, shift, far_q[...], keys, vals)
         return (dqueries * SCALE).astype(BF16), dkeys.astype(BF16), dvals.astype(BF16)
 
@@ -684,7 +689,6 @@
 def solution(mesh):
     small, halves, places, singles = tables()
     small, halves, places = (table.astype(BF16) for table in (small, halves, places))
-    unroll = 4
 
     def local(queries, key_rows, values, out_grad):
         rows, columns = queries.shape
@@ -749,7 +753,7 @@
             pltpu.SemaphoreType.DMA((COPIES,)),
         ]
         parts = pl.pallas_call(
-            functools.partial(kernel, heads, unroll),
+            functools.partial(kernel, heads),
             out_shape=(out,) * 4
             + (jax.ShapeDtypeStruct((32, columns), BF16), jax.ShapeDtypeStruct((64 * heads, 128), BF16)),
             in_specs=[anywhere] * 8,

time: 56 us -> 53.8 us (0.961)
  Pallas kernels: 55.2 us -> 53 us
    pallas_call x1, Pallas kernels: 52.5 us -> 50.3 us  [local(): pl.pallas_call(functools.partial(kernel, heads), out_shape=(out,) * 4 + (...]
where the time goes in v4:
time: 53.8 us; the launch traced here: 53.7 us
  Pallas kernels  53 us (99%)
  between operations  0.64 us (1%)
    pallas_call x1, Pallas kernels, local(): pl.pallas_call(functools.partial(kernel, heads), out_shape=(out,) * 4 + (...  50.3 us
    pallas_call x1, Pallas kernels, local(): pl.pallas_call(functools.partial(last_kernel, 2 * heads), out_shape=(out,...  2.71 us

profile of v4, /device:TPU:1, one launch (start us, length us, event | category | flops | bytes accessed | tf_op | source)
XLA Modules:
  0.0 53.7 jit_solution(3085981388170581944)
XLA Ops:
  0.6 50.3 %sibling_attention.1 = (bf16[64,2048]{1,0:T(8,128)(2,1)}, bf16[64,2048]{1,0:T(8,128)(2,1)}, bf16[64,2048]{1,0:T(8,128)(2,1)}, bf16[64,2048]{1,0:T(8,128)(2,1)}, ...) custom-call(bf16[64,2048]{1,0:T(8,128)(2,1)} %key_hbm.1, bf16[64,2048]{1,0:T(8,128)(2,1)} %value_hbm.1, ...), custom_call_target="tpu_custom_call" | custom-call | tf_op jit(solution)/shard_map/sibling_attention/pallas_call | solution.py:755
  51.0 2.7 %coarse_rows_added.1 = (bf16[64,2048]{1,0:T(8,128)(2,1)}, bf16[64,2048]{1,0:T(8,128)(2,1)}, bf16[64,2048]{1,0:T(8,128)(2,1)}, bf16[64,2048]{1,0:T(8,128)(2,1)}) custom-call(bf16[64,2048]{1,0:T(8,128)(2,1)} %get-tuple-element.10.att_ref, bf16[64,2048]{1,0:T(8,128)(2,1)} %get-tuple-element.11.dquery_ref, bf16[64,2048]{1,0:T(8,128)(2,1)} %get-tuple-element.12.dkey_ref, ...), custom_call_target="tpu_custom_call" | custom-call | tf_op jit(solution)/shard_map/coarse_rows_added/pallas_call | solution.py:768

commit v5 on v4

--- a/solution.py
+++ b/solution.py
@@ -21,6 +21,7 @@
 FAR = ((1, 0, 0, 64), (2, 64, 64, 32), (3, 64, 96, 32))
 FAR += tuple((n, 96, 128 + 16 * (n - 4), 16) for n in (4, 5, 6, 7))
 PLANE = 16
+PACK = 4
 
 
 def tables():
@@ -471,46 +472,54 @@
     forward_near()
     sums_back.wait_recv()
 
-    def combine(h):
-        cols = columns(h)
-        top_row = tops[h, pl.ds(0, 1)] + tops[h, pl.ds(1, 1)]
-        total_row = totals[h, pl.ds(0, 1)] + totals[h, pl.ds(1, 1)]
-        for group in (0, 1):
-            top_row = top_row + to_row(sums_recv[h, group, pl.ds(8, 8), pl.ds(0, 1)], 112 + 8 * group)
-            total_row = total_row + to_row(sums_recv[h, group, pl.ds(8, 8), pl.ds(64, 1)], 112 + 8 * group)
-        scores = local_scores[h]
-        coarse = single_tab[pl.ds(S_ANC, 128), everything] + top_row
-        top = jnp.max(jnp.maximum(scores, coarse), axis=1, keepdims=True)
-        expo = jnp.exp(scores - top)
-        factor = jnp.exp(coarse - top)
-        total = jnp.sum(expo + factor * total_row, axis=1, keepdims=True)
-        inverse = 1.0 / total
-        numer_all = jnp.concatenate(
-            [numer[h], sums_recv[h, 0, pl.ds(0, 8)], sums_recv[h, 1, pl.ds(0, 8)]], axis=0
-        ).astype(BF16)
-        outcome = (mm(expo.astype(BF16), rows_in[1, :, cols]) + mm(factor.astype(BF16), numer_all)) * inverse
-        att_buf[:, cols] = outcome.astype(BF16)
-        grad = rows_in[3, :, cols]
-        dots = jnp.sum(grad.astype(F32) * outcome, axis=1, keepdims=True)
-        probs = expo * inverse
-        weight = (factor * inverse).astype(BF16)
-        local_probs[h] = probs.astype(BF16)
-        local_ds[h] = (probs * (local_dprob[h] - dots)).astype(BF16)
+    def combine(every):
         lane = lax.broadcasted_iota(jnp.int32, (128, 128), 1)
-        dots_wide = jnp.broadcast_to(dots, (128, 128))
-        dots_high = dots_wide.astype(BF16).astype(F32)
-        dots_pair = jnp.where(lane < 64, dots_high, dots_wide - dots_high).astype(BF16)
-        both = mm_tn(weight, jnp.concatenate([grad, dots_pair], axis=1))
-        adj = both[:, 0:128]
-        shift = both[:, 128:256]
-        adjoint[h] = adj.astype(BF16)
-        offset[h] = shift
-        for group in (0, 1):
-            low = 112 + 8 * group
-            adj_send[h, group, pl.ds(0, 8)] = adj[low : low + 8]
-            adj_send[h, group, pl.ds(8, 8)] = shift[low : low + 8]
-
-    each_head(combine)
+        coarse = {}
+        total_row = {}
+        for h in every:
+            top_row = tops[h, pl.ds(0, 1)] + tops[h, pl.ds(1, 1)]
+            totals_row = totals[h, pl.ds(0, 1)] + totals[h, pl.ds(1, 1)]
+            for group in (0, 1):
+                top_row = top_row + to_row(sums_recv[h, group, pl.ds(8, 8), pl.ds(0, 1)], 112 + 8 * group)
+                totals_row = totals_row + to_row(sums_recv[h, group, pl.ds(8, 8), pl.ds(64, 1)], 112 + 8 * group)
+            coarse[h] = single_tab[pl.ds(S_ANC, 128), everything] + top_row
+            total_row[h] = totals_row
+        top = {h: jnp.max(jnp.maximum(local_scores[h], coarse[h]), axis=1, keepdims=True) for h in every}
+        expo = {h: jnp.exp(local_scores[h] - top[h]) for h in every}
+        factor = {h: jnp.exp(coarse[h] - top[h]) for h in every}
+        inverse = {h: 1.0 / jnp.sum(expo[h] + factor[h] * total_row[h], axis=1, keepdims=True) for h in every}
+        outcome = {}
+        for h in every:
+            numer_all = jnp.concatenate(
+                [numer[h], sums_recv[h, 0, pl.ds(0, 8)], sums_recv[h, 1, pl.ds(0, 8)]], axis=0
+            ).astype(BF16)
+            sums = mm(expo[h].astype(BF16), rows_in[1, :, columns(h)]) + mm(factor[h].astype(BF16), numer_all)
+            outcome[h] = sums * inverse[h]
+        dots = {}
+        for h in every:
+            att_buf[:, columns(h)] = outcome[h].astype(BF16)
+            dots[h] = jnp.sum(rows_in[3, :, columns(h)].astype(F32) * outcome[h], axis=1, keepdims=True)
+        for h in every:
+            dots_wide = jnp.broadcast_to(dots[h], (128, 128))
+            dots_high = dots_wide.astype(BF16).astype(F32)
+            dots_pair = jnp.where(lane < 64, dots_high, dots_wide - dots_high).astype(BF16)
+            weight = (factor[h] * inverse[h]).astype(BF16)
+            both = mm_tn(weight, jnp.concatenate([rows_in[3, :, columns(h)], dots_pair], axis=1))
+            adj = both[:, 0:128]
+            shift = both[:, 128:256]
+            adjoint[h] = adj.astype(BF16)
+            offset[h] = shift
+            for group in (0, 1):
+                low = 112 + 8 * group
+                adj_send[h, group, pl.ds(0, 8)] = adj[low : low + 8]
+                adj_send[h, group, pl.ds(8, 8)] = shift[low : low + 8]
+        for h in every:
+            probs = expo[h] * inverse[h]
+            local_probs[h] = probs.astype(BF16)
+            local_ds[h] = (probs * (local_dprob[h] - dots[h])).astype(BF16)
+
+    for first in range(0, heads, PACK):
+        combine(range(first, min(first + PACK, heads)))
     adj_out.start()
     stores[0].start()
     exits[0].start()
@@ -518,30 +527,37 @@
     def shift_of(h, start, count):
         return offset[h, pl.ds(start, count), pl.ds(0, 1)] + offset[h, pl.ds(start, count), pl.ds(64, 1)]
 
-    def backward_near(h):
-        cols = columns(h)
-        dqueries, dkeys, dvals = attend_back(
-            expo_near[h], adjoint[h, pl.ds(64, 48)], shift_of(h, 64, 48),
-            coarse_q[pl.ds(64, 48), cols], near_rows(0, h), near_rows(1, h),
-        )
-        dcoarse_q[h, pl.ds(64, 48)] = dqueries
-        for side in (0, 1):
-            part_grad[side, 0, :, cols] = dkeys[64 * side : 64 * side + 64].astype(BF16)
-            part_grad[side, 1, :, cols] = dvals[64 * side : 64 * side + 64].astype(BF16)
-
-    def backward_one(h):
-        cols = columns(h)
-        dqueries, dkeys, dvals = attend_back(
-            expo_one[h], adjoint[h, pl.ds(0, 64)], shift_of(h, 0, 64),
-            coarse_q[pl.ds(0, 64), cols], one_kv[0, :, cols], one_kv[1, :, cols],
-        )
-        dcoarse_q[h, pl.ds(0, 64)] = dqueries
-        one_part[0, :, cols] = dkeys.astype(BF16)
-        one_part[1, :, cols] = dvals.astype(BF16)
-
-    each_head(backward_near)
+    def backward_all(start, rows, keys_of, expo, put):
+        every = range(heads)
+        queries = [coarse_q[pl.ds(start, rows), columns(h)] for h in every]
+        inner = [
+            mm_nt(adjoint[h, pl.ds(start, rows)], keys_of(1, h)) - shift_of(h, start, rows) for h in every
+        ]
+        dscore = [(expo[h] * inner[h]).astype(BF16) for h in every]
+        dqueries = [mm(dscore[h], keys_of(0, h)) for h in every]
+        dkeys = [mm_tn(dscore[h], queries[h]) * SCALE for h in every]
+        dvals = [mm_tn(expo[h].astype(BF16), adjoint[h, pl.ds(start, rows)]) for h in every]
+        for h in every:
+            dcoarse_q[h, pl.ds(start, rows)] = dqueries[h]
+            put(h, 0, dkeys[h].astype(BF16))
+            put(h, 1, dvals[h].astype(BF16))
+
+    def backward_near():
+        def put(h, kv, rows):
+            part_grad[0, kv, :, columns(h)] = rows[0:64]
+            part_grad[1, kv, :, columns(h)] = rows[64:128]
+
+        backward_all(64, 48, near_rows, expo_near, put)
+
+    def backward_one():
+        def put(h, kv, rows):
+            one_part[kv, :, columns(h)] = rows
+
+        backward_all(0, 64, one_rows, expo_one, put)
+
+    backward_near()
     part_swap.start()
-    each_head(backward_one)
+    backward_one()
     one_back.start()
 
     def unpooled(rows):
@@ -568,21 +584,6 @@
     each_head(sum_near)
     for copy in near_back:
         copy.start()
-    one_back.wait_recv()
-
-    def local_back(h):
-        cols = columns(h)
-        dkeys = mm_tn(local_ds[h], rows_in[2, :, cols]) * SCALE
-        dvals = mm_tn(local_probs[h], rows_in[3, :, cols])
-        for kv, total in ((0, dkeys), (1, dvals)):
-            total = total + unpooled(one_recv[kv, :, cols].astype(F32))
-            dkv_buf[kv, :, cols] = total.astype(BF16)
-
-    each_head(local_back)
-    for i in (2, 3):
-        stores[i].start()
-        exits[i].start()
-
     adj_out.wait_recv()
 
     def backward_far(keys, vals, span):
@@ -598,6 +599,7 @@
         dqueries, dkeys, dvals = backward_far(pair_kv[:, everything], pair_kv[:, right], 128)
         rows = jnp.concatenate([dkeys, dvals, dqueries], axis=0)
         drows_send[...] = mm(place_tab[:, pl.ds(P_PICK, 384)], rows).astype(BF16)
+        drows_back.start()
 
     @pl.when(core == 1)
     def _():
@@ -607,6 +609,24 @@
         for copy in far_back:
             copy.start()
         dfar_q[...] = dqueries
+
+    one_back.wait_recv()
+
+    def local_back(h):
+        cols = columns(h)
+        dkeys = mm_tn(local_ds[h], rows_in[2, :, cols]) * SCALE
+        dvals = mm_tn(local_probs[h], rows_in[3, :, cols])
+        for kv, total in ((0, dkeys), (1, dvals)):
+            total = total + unpooled(one_recv[kv, :, cols].astype(F32))
+            dkv_buf[kv, :, cols] = total.astype(BF16)
+
+    each_head(local_back)
+    for i in (2, 3):
+        stores[i].start()
+        exits[i].start()
+
+    @pl.when(core == 1)
+    def _():
         for copy in far_back:
             copy.wait_recv()
         came = dfar_recv[...].astype(F32)
@@ -615,8 +635,7 @@
         rows = jnp.concatenate([came[0:64], level_six, level_seven, jnp.zeros((16, 256), F32)], axis=0).astype(BF16)
         rows = jnp.concatenate([dfar_q[...], rows[:, 0:128], rows[:, 128:256]], axis=0)
         drows_send[...] = mm(place_tab[:, pl.ds(P_FAR, 384)], rows).astype(BF16)
-
-    drows_back.start()
+        drows_back.start()
 
     for copy in near_back:
         copy.wait_recv()

time: 53.8 us -> 53.8 us (level)
  no operation moved by 1% of the time
where the time goes in v5:
time: 53.8 us; the launch traced here: 53.6 us
  Pallas kernels  53 us (99%)
  between operations  0.64 us (1%)
    pallas_call x1, Pallas kernels, local(): pl.pallas_call(functools.partial(kernel, heads), out_shape=(out,) * 4 + (...  50.3 us
    pallas_call x1, Pallas kernels, local(): pl.pallas_call(functools.partial(last_kernel, 2 * heads), out_shape=(out,...  2.71 us

profile of v5, /device:TPU:1, one launch (start us, length us, event | category | flops | bytes accessed | tf_op | source)
XLA Modules:
  0.0 53.6 jit_solution(14932567461627195871)
XLA Ops:
  0.6 50.3 %sibling_attention.1 = (bf16[64,2048]{1,0:T(8,128)(2,1)}, bf16[64,2048]{1,0:T(8,128)(2,1)}, bf16[64,2048]{1,0:T(8,128)(2,1)}, bf16[64,2048]{1,0:T(8,128)(2,1)}, ...) custom-call(bf16[64,2048]{1,0:T(8,128)(2,1)} %key_hbm.1, bf16[64,2048]{1,0:T(8,128)(2,1)} %value_hbm.1, ...), custom_call_target="tpu_custom_call" | custom-call | tf_op jit(solution)/shard_map/sibling_attention/pallas_call | solution.py:774
  50.9 2.7 %coarse_rows_added.1 = (bf16[64,2048]{1,0:T(8,128)(2,1)}, bf16[64,2048]{1,0:T(8,128)(2,1)}, bf16[64,2048]{1,0:T(8,128)(2,1)}, bf16[64,2048]{1,0:T(8,128)(2,1)}) custom-call(bf16[64,2048]{1,0:T(8,128)(2,1)} %get-tuple-element.10.att_ref, bf16[64,2048]{1,0:T(8,128)(2,1)} %get-tuple-element.11.dquery_ref, bf16[64,2048]{1,0:T(8,128)(2,1)} %get-tuple-element.12.dkey_ref, ...), custom_call_target="tpu_custom_call" | custom-call | tf_op jit(solution)/shard_map/coarse_rows_added/pallas_call | solution.py:787
